TPU v7x, 512 devices: a whole 4x4x16 slice. The times are simulated.
512 devices in a mesh: pair: 32 (over z, core), tau: 16 (over x, y).
Axes of the slice: x: 4, y: 4, z: 16, core: 2. Of those that a mesh axis runs over, the one named last changes fastest.
Arguments:
- coeff: bfloat16 [128, 128, 1024], P('pair'), may hold values from -6 to 6
- green_fwd: bfloat16 [1024, 16, 1024], P('pair', 'tau'), may hold values from -1 to 1
- green_bwd: bfloat16 [1024, 16, 1024], P('pair', 'tau'), may hold values from -1 to 1
- home_atom: int32 [1024], P('pair'), may hold values from 0 to 3, as said below
- send_atoms: int32 [1024], P('pair'), may hold values from 0 to 3, as said below
- partner: int32 [1024], P('pair'), may hold values from 0 to 31, as said below
- mirror: int32 [1024], P('pair'), may hold values from 0 to 1023, as said below
Outputs:
- response: float32 [1024, 16, 128, 128], P('pair', 'tau')
Inputs may be any that keep to these rules, and one draw needn't show every extreme that they name: mirror[mirror[p]] = p for every pair; a pair's mirror has the same local number on its index of pair as the pair on its own; at most 1 pairs of one index of pair have their mirror on any one index of pair, and this is reached in every draw. partner[p] is the index of pair that holds mirror[p]. `home_atom`: the first atom of mirror[p] is the second atom of p, and the second atom of mirror[p] is the first atom of p. send_atoms[partner[p] * 32 + d] = home_atom[mirror[p]] for every pair p on index d of pair.
All inputs are finite; a program needn't handle non-finite values.
Results may differ from a plain program's by a relative error of at most 0.004.
Values may be sent and summed in bfloat16 or wider, within the bound.
No kernel may reach another device: no remote copies, remote signals or barrier semaphores. Data moves between devices by JAX's collectives and lax.ppermute only.
A program may use at most 64 MiB of HBM per device.

v0:
```python
import jax
import jax.numpy as jnp
from jax import lax
from jax.sharding import PartitionSpec as P

AUX = 128
AO = 32


def body(coeff, green_fwd, green_bwd, home_atom, send_atoms, partner, mirror):
    peer_count = lax.axis_size("pair")
    outgoing = jnp.take(coeff, send_atoms, axis=0)
    remote = lax.all_to_all(outgoing, "pair", split_axis=0, concat_axis=0, tiled=True)
    pair_dev = home_atom.shape[0]
    tau_count = green_fwd.shape[1]
    block_size = 8
    block_count = pair_dev // block_size

    def block_work(block_items):
        home_block, partner_block, forward_block, backward_block = block_items
        coeff_first = jnp.take(coeff, home_block, axis=0).reshape(block_size, AUX, AO, AO)
        coeff_second = jnp.take(remote, partner_block, axis=0).reshape(block_size, AUX, AO, AO)
        forward = forward_block.reshape(block_size, tau_count, AO, AO)
        backward = backward_block.reshape(block_size, tau_count, AO, AO)
        left_part = jnp.einsum(
            "pxac,ptcb->ptxab", coeff_first, forward, preferred_element_type=jnp.float32
        ).astype(jnp.bfloat16)
        right_part = jnp.einsum(
            "ptad,pxdb->ptxab", backward, coeff_second, preferred_element_type=jnp.float32
        ).astype(jnp.bfloat16)
        left_flat = left_part.reshape(block_size, tau_count, AUX, AO * AO)
        right_flat = right_part.reshape(block_size, tau_count, AUX, AO * AO)
        return jnp.einsum(
            "ptxk,ptyk->ptxy", left_flat, right_flat, preferred_element_type=jnp.float32
        ) * (1.0 / AO)

    tiles = lax.map(
        block_work,
        (
            home_atom.reshape(block_count, block_size),
            partner.reshape(block_count, block_size),
            green_fwd.reshape(block_count, block_size, tau_count, AO * AO),
            green_bwd.reshape(block_count, block_size, tau_count, AO * AO),
        ),
    )
    tiles = tiles.reshape(pair_dev, tau_count, AUX, AUX)
    mirror_dev = mirror // pair_dev
    mirror_loc = mirror % pair_dev
    slot_count = max(1, pair_dev // peer_count)
    local_index = jnp.arange(pair_dev, dtype=jnp.int32)
    same_peer = mirror_dev[:, None] == mirror_dev[None, :]
    earlier = local_index[None, :] < local_index[:, None]
    send_rank = jnp.sum((same_peer & earlier).astype(jnp.int32), axis=1)
    send_pos = mirror_dev * slot_count + send_rank
    outbox = (
        jnp.zeros((peer_count * slot_count, tau_count, AUX, AUX), jnp.float32)
        .at[send_pos]
        .set(tiles)
    )
    arrived = lax.all_to_all(outbox, "pair", split_axis=0, concat_axis=0, tiled=True)
    lower_mirror = mirror_loc[None, :] < mirror_loc[:, None]
    recv_rank = jnp.sum((same_peer & lower_mirror).astype(jnp.int32), axis=1)
    recv_pos = mirror_dev * slot_count + recv_rank
    returned = jnp.take(arrived, recv_pos, axis=0)
    return tiles + jnp.swapaxes(returned, -1, -2)


def solution(mesh):
    placed = (
        P("pair", None, None),
        P("pair", "tau", None),
        P("pair", "tau", None),
        P("pair"),
        P("pair"),
        P("pair"),
        P("pair"),
    )
    return jax.shard_map(
        body, mesh=mesh, in_specs=placed, out_specs=P("pair", "tau", None, None), check_vma=False
    )
```

profile of v0, /device:TPU:60, one launch (start us, length us, event | category | flops | bytes accessed | tf_op | source)
XLA Modules:
  0.0 605.9 jit_solution(12956564438941908735)
XLA Ops:
  1.3 6.2 %gather_fusion.2 = bf16[32,128,1024]{2,1,0:T(8,128)(2,1)} fusion(bf16[4,128,1024]{2,1,0:T(8,128)(2,1)} %param.9, s32[1024]{0:T(1024)S(1)} %pad_clamp_fusion.3), kind=kCustom, calls=%fused_computation.2 | custom fusion | bytes 16777344 | tf_op jit(solution)/shard_map/jit(_take)/gather | solution.py:12
  7.5 7.5 %broadcast_select_fusion.1 = bf16[32,128,1024]{2,1,0:T(8,128)(2,1)} fusion(bf16[32,128,1024]{2,1,0:T(8,128)(2,1)} %gather_fusion.2, pred[32]{0:T(512)(128)(4,1)S(1)} %compare_and_fusion.5), kind=kLoop, calls=%fused_computation.34 | loop fusion | flops 4194304 | bytes 16777248 | tf_op jit(solution)/shard_map/jit(_take)/select_n | solution.py:12
  15.0 15.6 %all-to-all-start = ((bf16[32,128,1024]{2,1,0:T(8,128)(2,1)}), bf16[32,128,1024]{2,1,0:T(8,128)(2,1)}, u32[]{:S(2)}, u32[]{:S(2)}) async-start(bf16[32,128,1024]{2,1,0:T(8,128)(2,1)} %broadcast_select_fusion.1), calls=%async_computation | async-start | bytes 16777216 | tf_op jit(solution)/shard_map/all_to_all | solution.py:13
  31.0 369.5 %all-to-all-done = bf16[32,128,1024]{2,1,0:T(8,128)(2,1)} async-done(((bf16[32,128,1024]{2,1,0:T(8,128)(2,1)}), bf16[32,128,1024]{2,1,0:T(8,128)(2,1)}, u32[]{:S(2)}, u32[]{:S(2)}) %all-to-all-start) | async-done | bytes 8388640 | tf_op jit(solution)/shard_map/all_to_all | solution.py:13
  400.5 84.1 %while.10 = (s32[]{:T(128)}, f32[4,8,1,128,128]{4,3,1,2,0:T(8,128)}, bf16[4,8,1,1024]{3,1,2,0:T(8,128)(2,1)}, s32[4,8]{1,0:T(4,128)S(1)}, bf16[4,128,1024]{2,1,0...) while((s32[]{:T(128)}, ...), condition=%wide.region_1.2_spmd, body=%wide.region_0.1_spmd.sunk | while | flops 406980736 | bytes 38446024 | solution.py:37
  400.5 4.1 gather_fusion.1
  404.6 2.4 copy.66
  411.5 2.0 gather_fusion
  413.5 3.9 copy.65
  417.6 2.4 fusion.36
  421.5 4.1 gather_fusion.1
  425.6 2.4 copy.66
  432.5 2.0 gather_fusion
  434.5 3.9 copy.65
  438.6 2.4 fusion.36
  442.6 4.1 gather_fusion.1
  446.6 2.4 copy.66
  453.5 2.0 gather_fusion
  455.6 3.9 copy.65
  459.6 2.4 fusion.36
  463.6 4.1 gather_fusion.1
  467.7 2.4 copy.66
  474.6 2.0 gather_fusion
  476.6 3.9 copy.65
  480.6 2.4 fusion.36
  486.2 6.2 %scatter_fusion = f32[32,128,128]{2,1,0:T(8,128)} fusion(f32[32,128,128]{2,1,0:T(8,128)} %broadcast.107, s32[32]{0:T(128)S(1)} %compare_select_fusion.4, f32[32,128,128]{2,1,0:T(8,128)} %bitcast.21), kind=kCustom, calls=%fused_computation.4 | custom fusion | bytes 6291584 | tf_op jit(solution)/shard_map/scatter | solution.py:58
  492.4 4.5 all-to-all-start.1
  497.0 1.9 copy.48
  498.9 97.3 %all-to-all-done.1 = f32[32,1,128,128]{3,2,1,0:T(8,128)} async-done(((f32[32,1,128,128]{3,2,1,0:T(8,128)}), f32[32,1,128,128]{3,2,1,0:T(8,128)}, u32[]{:S(2)}, u32[]{:S(2)}) %all-to-all-start.1) | async-done | bytes 2097184 | tf_op jit(solution)/shard_map/all_to_all | solution.py:60
  596.2 3.6 gather_fusion.3
  599.8 3.2 bitcast_add_fusion
  603.0 2.9 copy.49
  (64 shorter events, 28.0 us)
Async XLA Ops:
  15.0 15.6 %copy-start.1 = (s32[32]{0:T(128)S(1)}, s32[32]{0:T(128)}, u32[]{:S(2)}) copy-start(s32[32]{0:T(128)} %param.12) | copy-start | bytes 388
  15.0 15.7 %copy-start.2 = (s32[32]{0:T(128)S(1)}, s32[32]{0:T(128)}, u32[]{:S(2)}) copy-start(s32[32]{0:T(128)} %param.14) | copy-start | bytes 388
  15.0 15.8 %copy-start.3 = (s32[32]{0:T(128)S(1)}, s32[32]{0:T(128)}, u32[]{:S(2)}) copy-start(s32[32]{0:T(128)} %param.15) | copy-start | bytes 388
  15.0 385.5 %copy-start = (bf16[4,128,1024]{2,1,0:T(8,128)(2,1)S(1)}, bf16[4,128,1024]{2,1,0:T(8,128)(2,1)}, u32[]{:S(2)}) copy-start(bf16[4,128,1024]{2,1,0:T(8,128)(2,1)} %param.9) | copy-start | bytes 3145732
  15.0 385.5 %all-to-all-start = ((bf16[32,128,1024]{2,1,0:T(8,128)(2,1)}), bf16[32,128,1024]{2,1,0:T(8,128)(2,1)}, u32[]{:S(2)}, u32[]{:S(2)}) async-start(bf16[32,128,1024]{2,1,0:T(8,128)(2,1)} %broadcast_select_fusion.1), calls=%async_computation | async-start | bytes 16777216 | tf_op jit(solution)/shard_map/all_to_all | solution.py:13
  492.4 103.8 %all-to-all-start.1 = ((f32[32,1,128,128]{3,2,1,0:T(8,128)}), f32[32,1,128,128]{3,2,1,0:T(8,128)}, u32[]{:S(2)}, u32[]{:S(2)}) async-start(f32[32,1,128,128]{3,2,1,0:T(8,128)} %bitcast.22), calls=%async_computation.1 | async-start | bytes 4194304 | tf_op jit(solution)/shard_map/all_to_all | solution.py:60
where the time goes:
time: 607 us; the launch traced here: 606 us
  waiting for transfers between devices  467 us (77%)
  local copies, waits for them, and re-layouts  79.4 us (13%)
  starting transfers between devices  20.1 us (3%)
  other arithmetic  19.8 us (3%)
  matrix products  19.5 us (3%)
    all_to_all x1, waiting for transfers between devices, body(): lax.all_to_all(outgoing, 'pair', split_axis=0, concat_axis=0, tiled=True)  370 us
    all_to_all x1, waiting for transfers between devices, body(): lax.all_to_all(outbox, 'pair', split_axis=0, concat_axis=0, tiled=True)  97.3 us
    gather x8, local copies, waits for them, and re-layouts, block_work(): jnp.take(remote, partner_block, axis=0).reshape(block_size, AUX, AO, AO)  25.9 us
    gather x8, local copies, waits for them, and re-layouts, block_work(): jnp.take(coeff, home_block, axis=0).reshape(block_size, AUX, AO, AO)  23.8 us
    all_to_all x1, starting transfers between devices, body(): lax.all_to_all(outgoing, 'pair', split_axis=0, concat_axis=0, tiled=True)  15.6 us
  transfers between devices with their start and end apart: 2, of which 2 were waited for; matrix products, arithmetic and copies ran while one was open for 0% of the time, Pallas kernels for 0%

commit v1 on v0

v1 whole, which is shorter than its diff:
```python
import jax
import jax.numpy as jnp
import numpy as np
from jax import lax
from jax.experimental import pallas as pl
from jax.experimental.pallas import tpu as pltpu
from jax.sharding import PartitionSpec as P

AUX = 128
AO = 32
F32 = jnp.float32
BF16 = jnp.bfloat16


def dot(a, b):
    return jnp.dot(a, b, preferred_element_type=F32)


def compute_kernel(home_ref, ci_ref, rb_ref, eg_ref, eh_ref, out_ref, st, cit, cjn, cjt, gw1, gw2, hm1, hm2):
    taus = 16
    ci = ci_ref[0]

    def swap_minor(src_rows):
        parts = [src_rows[pl.ds(w, AO, stride=AO), :] for w in range(AO)]
        return parts

    for c in range(8):
        st[pl.ds(c * 128, 128), :] = ci[:, c * 128:(c + 1) * 128].astype(F32).T
    for c in range(8):
        rows = jnp.concatenate([st[pl.ds(c * 4 + w, AO, stride=AO), :] for w in range(4)], axis=0)
        cit[:, c * 128:(c + 1) * 128] = rows.T.astype(BF16)
    cj = rb_ref[:, 0, :, :1024].astype(F32).reshape(AUX, 1024)
    for c in range(8):
        st[pl.ds(c * 128, 128), :] = cj[:, c * 128:(c + 1) * 128].T
    for c in range(4):
        cjn[:, c * 128:(c + 1) * 128] = st[pl.ds(c * 256, 256), :].astype(BF16)
    for w in range(AO):
        hi, lo = w // 8, w % 8
        cjt[lo * 32:(lo + 1) * 32, hi * 128:(hi + 1) * 128] = st[pl.ds(w, AO, stride=AO), :].astype(BF16)
    row32 = lax.broadcasted_iota(jnp.int32, (32, 128), 0) // 8
    lane32 = lax.broadcasted_iota(jnp.int32, (32, 128), 1) // 32
    keep = row32 == lane32
    eg = eg_ref[...]
    eh = eh_ref[...]

    def unpack(lo, e, dst):
        packed = rb_ref[:, 0, :, lo:lo + 128].astype(F32)
        rep = jnp.concatenate([packed] * 4, axis=1)
        rep = jnp.where(keep[None], rep, 0.0).reshape(taus * 32, 128).astype(BF16)
        dst[...] = dot(rep, e).reshape(taus, 32, 256)

    unpack(1024, eh, hm2)
    unpack(1152, eg, gw2)
    unpack(1280, eg, gw1)
    unpack(1408, eh, hm1)

    wrow = lax.broadcasted_iota(jnp.int32, (256, 256), 0)
    wlane = lax.broadcasted_iota(jnp.int32, (256, 256), 1)
    wmask = (wrow // 32) == (wlane % 8)
    mmask = ((wrow // 8) % 8) == (wlane // 32)

    def step(t, carry):
        g1 = gw1[t]
        g2 = gw2[t]
        h1 = hm1[t]
        h2 = hm2[t]

        def wide(g):
            return jnp.where(wmask, jnp.concatenate([g] * 8, axis=0), 0.0).astype(BF16)

        def tall(h):
            return jnp.where(
                mmask, jnp.concatenate([h[a * 8:(a + 1) * 8] for a in range(4) for _ in range(8)], axis=0), 0.0
            ).astype(BF16)

        w1, w2, m1, m2 = wide(g1), wide(g2), tall(h1), tall(h2)
        y1 = dot(m1, cjt[...]).astype(BF16)
        y2 = dot(m2, cjn[...]).astype(BF16)
        acc = jnp.zeros((AUX, AUX), F32)
        for c in range(4):
            cols = slice(c * 256, (c + 1) * 256)
            x1 = dot(ci_ref[0, :, cols], w1).astype(BF16)
            r1 = jnp.concatenate([y1[c * 64:(c + 1) * 64, h * 128:(h + 1) * 128] for h in range(4)], axis=0)
            acc = acc + dot(x1, r1)
            x2 = dot(cit[:, cols], w2).astype(BF16)
            r2 = jnp.concatenate([y2[c * 64:(c + 1) * 64, h * 128:(h + 1) * 128] for h in range(4)], axis=0)
            acc = acc + dot(x2, r2)
        out_ref[t, 0] = (acc * (1.0 / AO)).astype(BF16)
        return carry

    lax.fori_loop(0, taus, step, 0)


def expand_constants():
    i = np.arange(128)[:, None]
    j = np.arange(256)[None, :]
    eg = ((i % 32) == (j // 8)).astype(np.float32)
    eh = ((i % 32) == (j % 32)).astype(np.float32)
    return jnp.asarray(eg, BF16), jnp.asarray(eh, BF16)


def compute(home2, coeff, rb):
    eg, eh = expand_constants()
    taus = 16
    return pl.pallas_call(
        compute_kernel,
        grid_spec=pltpu.PrefetchScalarGridSpec(
            num_scalar_prefetch=1,
            grid=(2,),
            in_specs=[
                pl.BlockSpec((1, AUX, 1024), lambda m, home: (home[m], 0, 0)),
                pl.BlockSpec((taus, 1, 8, 1536), lambda m, home: (0, m, 0, 0)),
                pl.BlockSpec((128, 256), lambda m, home: (0, 0)),
                pl.BlockSpec((128, 256), lambda m, home: (0, 0)),
            ],
            out_specs=pl.BlockSpec((taus, 1, AUX, AUX), lambda m, home: (0, m, 0, 0)),
            scratch_shapes=[
                pltpu.VMEM((1024, 128), F32),
                pltpu.VMEM((128, 1024), BF16),
                pltpu.VMEM((256, 512), BF16),
                pltpu.VMEM((256, 512), BF16),
                pltpu.VMEM((taus, 32, 256), F32),
                pltpu.VMEM((taus, 32, 256), F32),
                pltpu.VMEM((taus, 32, 256), F32),
                pltpu.VMEM((taus, 32, 256), F32),
            ],
        ),
        out_shape=jax.ShapeDtypeStruct((taus, 2, AUX, AUX), BF16),
        cost_estimate=pl.CostEstimate(flops=26_000_000_000, bytes_accessed=3_000_000, transcendentals=0),
    )(home2, coeff, rb, eg, eh)


def body(coeff, green_fwd, green_bwd, home_atom, send_atoms, partner, mirror):
    taus = lax.axis_size("tau")
    k = lax.axis_index("tau")
    fwd = green_fwd[:, 0, :].reshape(32, 1, 1024)
    bwd = green_bwd[:, 0, :].reshape(32, 1, 1024)
    g = jnp.concatenate([fwd, bwd], axis=1)
    own = g.reshape(32, 2, 4, 8, 32).transpose(0, 3, 1, 2, 4).reshape(32, 8, 256)
    turned = g.reshape(32, 2, 32, 4, 8).transpose(0, 4, 1, 3, 2).reshape(32, 8, 256)
    index = jnp.arange(32, dtype=jnp.int32)
    inverse = jnp.sum(jnp.where(partner[None, :] == index[:, None], index[None, :], 0), axis=1)
    slices = lax.dynamic_slice(coeff, (0, k * 8, 0), (4, 8, 1024))
    send_a = jnp.concatenate(
        [jnp.take(slices, send_atoms, axis=0, mode="clip"), jnp.take(turned, inverse, axis=0, mode="clip")], axis=2
    )
    got_a = lax.all_to_all(send_a, "pair", split_axis=0, concat_axis=0, tiled=True)
    send_b = jnp.concatenate([jnp.take(got_a, partner, axis=0, mode="clip"), own], axis=2)
    got_b = lax.all_to_all(send_b, "tau", split_axis=0, concat_axis=0, tiled=True)
    home2 = lax.dynamic_slice(home_atom, (k * 2,), (2,))
    tiles = compute(home2, coeff, got_b.reshape(taus, 2, 8, 1536))
    back = lax.all_to_all(tiles.reshape(32, AUX, AUX), "tau", split_axis=0, concat_axis=0, tiled=True)
    return back.astype(F32).reshape(32, 1, AUX, AUX)


def solution(mesh):
    placed = (
        P("pair", None, None),
        P("pair", "tau", None),
        P("pair", "tau", None),
        P("pair"),
        P("pair"),
        P("pair"),
        P("pair"),
    )
    return jax.shard_map(
        body, mesh=mesh, in_specs=placed, out_specs=P("pair", "tau", None, None), check_vma=False
    )
```

time: 607 us -> 137 us (0.23)
  the two profiles are of different devices: /device:TPU:60 before, /device:TPU:8 now
where the time goes in v1:
time: 137 us; the launch traced here: 136 us
  waiting for transfers between devices  50.8 us (37%)
  Pallas kernels  30.2 us (22%)
  starting transfers between devices  23 us (17%)
  blocking collectives  19.4 us (14%)
  local copies, waits for them, and re-layouts  8.54 us (6%)
  other arithmetic  4.16 us (3%)
    all_to_all x1, waiting for transfers between devices, body(): lax.all_to_all(send_a, 'pair', split_axis=0, concat_axis=0, tiled=True)  38.3 us
    pallas_call x1, Pallas kernels, compute(): pl.pallas_call(compute_kernel, grid_spec=pltpu.PrefetchScalarGridSpec(num...  30.2 us
    all_to_all x1, blocking collectives, body(): lax.all_to_all(tiles.reshape(32, AUX, AUX), 'tau', split_axis=0, concat_a...  19.4 us
    all_to_all x1, starting transfers between devices, body(): lax.all_to_all(send_a, 'pair', split_axis=0, concat_axis=0, tiled=True)  15.6 us
    all_to_all x1, waiting for transfers between devices, body(): lax.all_to_all(send_b, 'tau', split_axis=0, concat_axis=0, tiled=True)  12.5 us
    all_to_all x1, starting transfers between devices, body(): lax.all_to_all(send_b, 'tau', split_axis=0, concat_axis=0, tiled=True)  7.39 us
  transfers between devices with their start and end apart: 2, of which 2 were waited for; matrix products, arithmetic and copies ran while one was open for 1% of the time, Pallas kernels for 0%

profile of v1, /device:TPU:8, one launch (start us, length us, event | category | flops | bytes accessed | tf_op | source)
XLA Modules:
  0.0 136.3 jit_solution(731553541290866223)
XLA Ops:
  0.0 0.0 copy-start.1
  0.0 0.8 select_reduce_fusion
  0.8 0.9 constant_dynamic-update-slice_fusion.1
  1.6 0.8 constant_dynamic-update-slice_fusion
  2.5 0.3 copy.17
  2.8 1.1 copy.18
  3.8 0.4 reshape.26
  4.2 0.0 copy-done.1
  4.2 0.9 constant_dynamic-slice_fusion
  5.1 0.6 gather_fusion
  5.7 0.6 gather_fusion.1
  6.2 0.9 pad_maximum_fusion.1
  7.1 0.0 copy-start.2
  7.1 15.6 %all-to-all-start = ((bf16[32,8,1280]{2,1,0:T(8,128)(2,1)}), bf16[32,8,1280]{2,1,0:T(8,128)(2,1)S(1)}, u32[]{:S(2)}, u32[]{:S(2)}) async-start(bf16[32,8,1280]{2,1,0:T(8,128)(2,1)} %pad_maximum_fusion.1), calls=%async_computation | async-start | bytes 1310720 | tf_op jit(solution)/shard_map/all_to_all | solution.py:147
  22.7 0.4 reshape.27
  23.1 0.3 copy.19
  23.4 0.4 reshape.28
  23.8 0.0 copy-done.2
  23.8 38.3 %all-to-all-done = bf16[32,8,1280]{2,1,0:T(8,128)(2,1)S(1)} async-done(((bf16[32,8,1280]{2,1,0:T(8,128)(2,1)}), bf16[32,8,1280]{2,1,0:T(8,128)(2,1)S(1)}, u32[]{:S(2)}, u32[]{:S(2)}) %all-to-all-start) | async-done | bytes 655392 | tf_op jit(solution)/shard_map/all_to_all | solution.py:147
  62.1 0.6 gather_fusion.2
  62.7 0.0 copy-start.3
  62.7 0.9 pad_maximum_fusion
  63.7 7.4 %all-to-all-start.1 = ((bf16[32,8,1536]{2,1,0:T(8,128)(2,1)}), bf16[32,8,1536]{2,1,0:T(8,128)(2,1)S(1)}, u32[]{:S(2)}, u32[]{:S(2)}) async-start(bf16[32,8,1536]{2,1,0:T(8,128)(2,1)} %pad_maximum_fusion), calls=%async_computation.1 | async-start | bytes 1572864 | tf_op jit(solution)/shard_map/all_to_all | solution.py:149
  71.0 0.0 copy-done.3
  71.0 0.7 dynamic_slice.6.home_ref
  71.7 12.5 %all-to-all-done.1 = bf16[32,8,1536]{2,1,0:T(8,128)(2,1)S(1)} async-done(((bf16[32,8,1536]{2,1,0:T(8,128)(2,1)}), bf16[32,8,1536]{2,1,0:T(8,128)(2,1)S(1)}, u32[]{:S(2)}, u32[]{:S(2)}) %all-to-all-start.1) | async-done | bytes 786464 | tf_op jit(solution)/shard_map/all_to_all | solution.py:149
  84.2 0.0 copy-start
  84.2 0.9 copy-done
  85.1 30.2 %shard_map.82 = bf16[16,2,128,128]{3,2,1,0:T(8,128)(2,1)} custom-call(s32[2]{0:T(128)} %dynamic_slice.6.home_ref, bf16[4,128,1024]{2,1,0:T(8,128)(2,1)} %ci_ref.1, bf16[16,2,8,1536]{3,2,1,0:T(8,128)(2,1)} %bitcast.14, bf16[128,256]{1,0:T(8,128)(2,1)} %constant.18.clone.eg_ref, bf16[128,256]{1,0:T(8,128)(2,1)} %constant.19.clone.eh_ref), custom_call_target="tpu_custom_call" | custom-call | flops 25999998976 | bytes 3000000 | tf_op jit(solution)/shard_map/pallas_call | solution.py:105
  115.3 19.4 %all_to_all.15 = bf16[32,128,128]{2,1,0:T(8,128)(2,1)S(1)} all-to-all(bf16[32,128,128]{2,1,0:T(8,128)(2,1)} %bitcast.13), channel_id=1, replica_groups=mesh['pair'=32,'tau'=16] {'tau'}, dimensions={0} | all-to-all | bytes 2097152 | tf_op jit(solution)/shard_map/all_to_all | solution.py:152
  134.7 1.6 %bitcast_convert_fusion = f32[32,1,128,128]{3,2,1,0:T(8,128)} fusion(bf16[32,128,128]{2,1,0:T(8,128)(2,1)S(1)} %all_to_all.15), kind=kLoop, calls=%fused_computation.3 | loop fusion | flops 524288 | bytes 3145728 | tf_op jit(solution)/shard_map/reshape | solution.py:153
  (2 shorter events, 0.0 us)
Async XLA Ops:
  0.0 4.2 %copy-start.1 = (s32[32]{0:T(128)S(1)}, s32[32]{0:T(128)}, u32[]{:S(2)}) copy-start(s32[32]{0:T(128)} %param.13) | copy-start | bytes 388
  7.1 16.6 %copy-start.2 = (s32[32]{0:T(128)S(1)}, s32[32]{0:T(128)}, u32[]{:S(2)}) copy-start(s32[32]{0:T(128)} %param.14) | copy-start | bytes 388
  7.1 55.0 %all-to-all-start = ((bf16[32,8,1280]{2,1,0:T(8,128)(2,1)}), bf16[32,8,1280]{2,1,0:T(8,128)(2,1)S(1)}, u32[]{:S(2)}, u32[]{:S(2)}) async-start(bf16[32,8,1280]{2,1,0:T(8,128)(2,1)} %pad_maximum_fusion.1), calls=%async_computation | async-start | bytes 1310720 | tf_op jit(solution)/shard_map/all_to_all | solution.py:147
  62.7 8.3 %copy-start.3 = (s32[32]{0:T(128)S(1)}, s32[32]{0:T(128)}, u32[]{:S(2)}) copy-start(s32[32]{0:T(128)} %param.12) | copy-start | bytes 388
  63.7 20.5 %all-to-all-start.1 = ((bf16[32,8,1536]{2,1,0:T(8,128)(2,1)}), bf16[32,8,1536]{2,1,0:T(8,128)(2,1)S(1)}, u32[]{:S(2)}, u32[]{:S(2)}) async-start(bf16[32,8,1536]{2,1,0:T(8,128)(2,1)} %pad_maximum_fusion), calls=%async_computation.1 | async-start | bytes 1572864 | tf_op jit(solution)/shard_map/all_to_all | solution.py:149
  84.2 0.9 copy-start

commit v2 on v0

v2 whole, which is shorter than its diff:
```python
import functools

import jax
import jax.numpy as jnp
import numpy as np
from jax import lax
from jax.experimental import pallas as pl
from jax.experimental.pallas import tpu as pltpu
from jax.sharding import PartitionSpec as P


AUX = 128
AO = 32
CHIPS = 16
N_PAIR = 32
N_TAU = 16
F32 = jnp.float32
BF16 = jnp.bfloat16
BOTH = ("pair", "tau")


STEPS = (
    (1, 7, -7, -1), (7, -7, -1, 1), (-7, -1, 1, 7), (-1, 1, 7, -7),
    (2, -2, 6, -6), (-2, 2, -6, 6), (6, -6, 2, -2), (-6, 6, -2, 2),
    (3, -3, -5, 5), (-3, -5, 5, 3), (5, 3, -3, -5), (-5, 5, 3, -3),
    (0, 4, 8, -4), (4, 8, -4, 0), (8, -4, 0, 4), (-4, 0, 4, 8),
)


def routes():
    dst = np.zeros((CHIPS, N_TAU), np.int32)
    src = np.zeros((CHIPS, N_TAU), np.int32)
    column = np.zeros((CHIPS, CHIPS), np.int32)
    for z in range(CHIPS):
        for k in range(N_TAU):
            to = (z + STEPS[k][z % 4]) % CHIPS
            dst[z, k] = to
            src[to, k] = z
            column[to, z] = k
    along_z = [
        ((2 * z + core) * N_TAU + k, (2 * int(dst[z, k]) + core) * N_TAU + k)
        for z in range(CHIPS)
        for core in range(2)
        for k in range(N_TAU)
    ]
    return dst, src, column, along_z


DST, SRC, COLUMN, ALONG_Z = routes()
SWAP = [(i, i ^ 1) for i in range(N_PAIR)]


def dot(a, b):
    return jnp.dot(a, b, preferred_element_type=F32)


VM = pl.BlockSpec(memory_space=pltpu.VMEM)
SM = pl.BlockSpec(memory_space=pltpu.SMEM)


def prepare_kernel(
    spot_ref, partner_ref, asked_ref, homes_ref, dst_ref, src_ref, near_ref, away_ref, peers_ref, coeff_ref, gf_ref,
    gb_ref, send_ref, atom0_ref, atom1_ref, home_ref, wide
):
    p, k = spot_ref[0], spot_ref[1]
    z, core = p // 2, p % 2
    to = 2 * dst_ref[z * N_TAU + k]
    come = 2 * src_ref[z * N_TAU + k]
    for j, atom_ref in enumerate((atom0_ref, atom1_ref)):
        side = core if j == 0 else 1 - core
        atom_ref[0] = coeff_ref[asked_ref[to + side]]
        found = jnp.int32(0)
        for m in range(N_PAIR):
            found = jnp.where(partner_ref[m] == come + side, homes_ref[m], found)
        home_ref[j] = found
    eye = lax.broadcasted_iota(jnp.int32, (32, 32), 0) == lax.broadcasted_iota(jnp.int32, (32, 32), 1)
    peers = peers_ref[...]

    def pick(table_ref):
        row = table_ref[pl.ds(p, 1), :]
        column = jnp.sum(jnp.where(eye, jnp.broadcast_to(row, (32, 32)), 0.0), axis=1, keepdims=True)
        return jnp.where(column == peers, 1.0, 0.0).astype(BF16)

    near, away = pick(near_ref), pick(away_ref)
    mine = jnp.concatenate([dot(near, gf_ref[...]), dot(near, gb_ref[...])], axis=0).astype(BF16)
    theirs = [dot(away, gf_ref[...]), dot(away, gb_ref[...])]
    for c in range(4):
        r = lax.broadcasted_iota(jnp.int32, (1024, 256), 0)
        q = lax.broadcasted_iota(jnp.int32, (1, 256), 1) + 256 * c
        source = (q % 32) * 32 + ((q // 32) % 4) * 8 + q // 128
        turn = jnp.where(r == source, 1.0, 0.0).astype(BF16)
        flipped = dot(mine, turn)
        for i in range(2):
            for kind in range(2):
                wide[:, 2 * c + i, kind * 128:(kind + 1) * 128] = flipped[
                    kind * 32:(kind + 1) * 32, i * 128:(i + 1) * 128
                ]
    for kind in range(2):
        for lo in range(8):
            wide[:, lo, 256 + kind * 128:256 + (kind + 1) * 128] = jnp.concatenate(
                [theirs[kind][:, (hi * 8 + lo) * 32:(hi * 8 + lo + 1) * 32] for hi in range(4)], axis=1
            )
    send_ref[...] = wide[...].astype(BF16)


def prepare(spot, partner, send_atoms, home_atom, coeff, fwd, bwd):
    sides = np.arange(N_PAIR) % 2
    near = np.zeros((N_PAIR, N_PAIR), np.float32)
    away = np.zeros((N_PAIR, N_PAIR), np.float32)
    for p in range(N_PAIR):
        for j in range(2):
            near[p, j::2] = 2 * SRC[p // 2] + (sides[p] ^ j)
            away[p, j::2] = 2 * DST[p // 2] + (sides[p] ^ j)
    return pl.pallas_call(
        prepare_kernel,
        in_specs=[SM] * 6 + [VM] * 6,
        out_specs=[VM, VM, VM, SM],
        scratch_shapes=[pltpu.VMEM((32, 8, 512), F32)],
        out_shape=[
            jax.ShapeDtypeStruct((32, 8, 512), BF16),
            jax.ShapeDtypeStruct((1, AUX, 1024), BF16),
            jax.ShapeDtypeStruct((1, AUX, 1024), BF16),
            jax.ShapeDtypeStruct((2,), jnp.int32),
        ],
        cost_estimate=pl.CostEstimate(flops=200_000_000, bytes_accessed=3_000_000, transcendentals=0),
    )(
        spot,
        partner,
        send_atoms,
        home_atom,
        jnp.asarray(DST.reshape(-1)),
        jnp.asarray(SRC.reshape(-1)),
        jnp.asarray(near),
        jnp.asarray(away),
        partner.astype(F32).reshape(1, N_PAIR),
        coeff,
        fwd,
        bwd,
    )


UNROLL = 8


def z_kernel(slot, home_ref, ci_ref, own_ref, far_ref, eg_ref, eh_ref, z_ref, cin, fb, bb, s_a, s_b):
    for c in range(4):
        cin[:, c * 128:(c + 1) * 128] = ci_ref[home_ref[slot], :, c * 256:(c + 1) * 256].astype(F32).T.astype(BF16)
    keep = (lax.broadcasted_iota(jnp.int32, (64, 128), 0) // 16) == (lax.broadcasted_iota(jnp.int32, (64, 128), 1) // 32)

    def unpack(packed, e, dst, kind):
        rep = jnp.concatenate([packed.astype(F32)] * 8, axis=1)
        rep = jnp.where(keep[None], rep, 0.0).reshape(N_TAU * 64, 128).astype(BF16)
        dst[:, kind] = dot(rep, e).astype(BF16).reshape(N_TAU, 64, 256)

    unpack(own_ref[:, slot, :, 0:128], eh_ref[...], fb, 0)
    unpack(far_ref[0, :, :, 0:128], eh_ref[...], fb, 1)
    unpack(own_ref[:, slot, :, 128:256], eg_ref[...], bb, 0)
    unpack(far_ref[0, :, :, 128:256], eg_ref[...], bb, 1)
    row = lax.broadcasted_iota(jnp.int32, (64, 256), 0) // 8
    lane = lax.broadcasted_iota(jnp.int32, (64, 256), 1)
    mask_minor = jnp.where(row == lane // 32, 1.0, 0.0).astype(BF16)
    mask_major = jnp.where(row == lane % 8, 1.0, 0.0).astype(BF16)

    def spread(h, mask):
        return jnp.concatenate(
            [jnp.concatenate([h[a * 16:(a + 1) * 16]] * 4, axis=0) * mask for a in range(4)], axis=0
        )

    def first(t, buf):
        for kind in range(2):
            s1 = dot(spread(fb[t, kind], mask_minor), cin[...]).astype(BF16)
            for h in range(4):
                for a in range(4):
                    buf[kind * 256 + a * 64:kind * 256 + (a + 1) * 64, h * 128:(h + 1) * 128] = s1[
                        h * 64:(h + 1) * 64, a * 128:(a + 1) * 128
                    ]

    def second(t, buf):
        m2 = jnp.concatenate([spread(bb[t, 0], mask_major), spread(bb[t, 1], mask_major)], axis=1)
        for h in range(2):
            z = dot(m2, buf[:, h * 256:(h + 1) * 256])
            z_ref[t, :, h * 512:h * 512 + 256] = z[:, :128].T.astype(BF16)
            z_ref[t, :, h * 512 + 256:h * 512 + 512] = z[:, 128:].T.astype(BF16)

    first(0, s_a)

    def step(i, carry):
        for u in range(0, UNROLL, 2):
            t = UNROLL * i + u
            first(t + 1, s_b)
            second(t, s_a)
            first(jnp.minimum(t + 2, N_TAU - 1), s_a)
            second(t + 1, s_b)
        return carry

    lax.fori_loop(0, N_TAU // UNROLL, step, 0)


def apply_z(slot, home, coeff, own, far, eg, eh):
    return pl.pallas_call(
        functools.partial(z_kernel, slot),
        in_specs=[SM, VM, VM, VM, VM, VM],
        out_specs=VM,
        scratch_shapes=[pltpu.VMEM((256, 512), BF16)]
        + [pltpu.VMEM((N_TAU, 2, 64, 256), BF16)] * 2
        + [pltpu.VMEM((512, 512), BF16)] * 2,
        out_shape=jax.ShapeDtypeStruct((N_TAU, AUX, 1024), BF16),
        compiler_params=pltpu.CompilerParams(vmem_limit_bytes=16 * 2**20),
        cost_estimate=pl.CostEstimate(flops=8_000_000_000, bytes_accessed=5_000_000, transcendentals=0),
    )(home, coeff, own, far, eg, eh)


def last_kernel(c0_ref, c1_ref, z0_ref, z1_ref, pm_ref, out_ref, cp):
    for j, ref in enumerate((c0_ref, c1_ref)):
        turned = [dot(ref[0, :, a * 256:(a + 1) * 256], pm_ref[...]) for a in range(4)]
        for h in range(4):
            cp[j, :, h * 256:(h + 1) * 256] = jnp.concatenate(
                [turned[a][:, h * 64:(h + 1) * 64] for a in range(4)], axis=1
            ).astype(BF16)

    def step(i, carry):
        for j, ref in enumerate((z0_ref, z1_ref)):
            acc = lax.dot_general(
                ref[pl.ds(4 * i, 4)].reshape(4 * AUX, 1024),
                cp[j],
                (((1,), (1,)), ((), ())),
                preferred_element_type=F32,
            )
            out_ref[pl.ds(4 * i, 4), j] = (acc * (1.0 / AO)).astype(BF16).reshape(4, AUX, AUX)
        return carry

    lax.fori_loop(0, N_TAU // 4, step, 0)


def last_product(c0, c1, z0, z1, pm):
    return pl.pallas_call(
        last_kernel,
        in_specs=[VM] * 5,
        out_specs=VM,
        scratch_shapes=[pltpu.VMEM((2, AUX, 1024), BF16)],
        out_shape=jax.ShapeDtypeStruct((N_TAU, 2, AUX, AUX), BF16),
        compiler_params=pltpu.CompilerParams(vmem_limit_bytes=16 * 2**20),
        cost_estimate=pl.CostEstimate(flops=1_200_000_000, bytes_accessed=10_000_000, transcendentals=0),
    )(c0, c1, z0, z1, pm)


def finish_kernel(spot_ref, partner_ref, column_ref, in_ref, out_ref):
    base = pl.program_id(0) * 8
    p = spot_ref[0]
    for i in range(8):
        other = partner_ref[base + i]
        place = 2 * column_ref[(p // 2) * CHIPS + other // 2] + (p + other) % 2
        out_ref[i] = in_ref[place].astype(F32)


def finish(spot, partner, tiles):
    return pl.pallas_call(
        finish_kernel,
        grid=(4,),
        in_specs=[SM, SM, SM, VM],
        out_specs=pl.BlockSpec((8, AUX, AUX), lambda i: (i, 0, 0)),
        out_shape=jax.ShapeDtypeStruct((32, AUX, AUX), F32),
        compiler_params=pltpu.CompilerParams(vmem_limit_bytes=8 * 2**20),
        cost_estimate=pl.CostEstimate(flops=1_000_000, bytes_accessed=3_000_000, transcendentals=0),
    )(spot, partner, jnp.asarray(COLUMN.reshape(-1)), tiles)


def constants():
    i = np.arange(128)[:, None]
    j = np.arange(256)[None, :]
    eg = ((i % 32) == (j // 8)).astype(np.float32)
    eh = ((i % 32) == (j % 32)).astype(np.float32)
    r = np.arange(256)[:, None]
    lo, b = r // 32, r % 32
    pm = (j == (b // 8) * 64 + (b % 8) * 8 + lo).astype(np.float32)
    return jnp.asarray(eg, BF16), jnp.asarray(eh, BF16), jnp.asarray(pm, BF16)


def exchange(x):
    return lax.all_to_all(x, "tau", split_axis=0, concat_axis=0, tiled=True)


def body(coeff, green_fwd, green_bwd, home_atom, send_atoms, partner, mirror):
    spot = jnp.stack([lax.axis_index("pair"), lax.axis_index("tau")]).astype(jnp.int32)
    eg, eh, pm = constants()
    send, atom0, atom1, home = prepare(
        spot, partner, send_atoms, home_atom, coeff, green_fwd[:, 0, :], green_bwd[:, 0, :]
    )
    c0 = lax.ppermute(atom0, BOTH, ALONG_Z)
    greens = exchange(send).reshape(N_TAU, 2, 8, 512)
    outgoing, atom1 = lax.optimization_barrier((greens[:, :, :, 256:512].transpose(1, 0, 2, 3), atom1))
    far = lax.ppermute(outgoing, BOTH, ALONG_Z)
    other_far = lax.ppermute(far[1:2], "pair", SWAP)
    c1 = lax.ppermute(atom1, BOTH, ALONG_Z)
    c1 = lax.ppermute(c1, "pair", SWAP)
    z0 = apply_z(0, home, coeff, greens, far, eg, eh)
    z1 = apply_z(1, home, coeff, greens, other_far, eg, eh)
    tiles = last_product(c0, c1, z0, z1, pm)
    back = exchange(tiles.reshape(32, AUX, AUX))
    return finish(spot, partner, back).reshape(32, 1, AUX, AUX)


def solution(mesh):
    placed = (
        P("pair", None, None),
        P("pair", "tau", None),
        P("pair", "tau", None),
        P("pair"),
        P("pair"),
        P("pair"),
        P("pair"),
    )
    return jax.shard_map(
        body, mesh=mesh, in_specs=placed, out_specs=P("pair", "tau", None, None), check_vma=False
    )
```

time: 607 us -> 116 us (0.19)
  the two profiles are of different devices: /device:TPU:60 before, /device:TPU:1 now
where the time goes in v2:
time: 116 us
  blocking collectives  55.5 us (48%)
  starting transfers between devices  33.4 us (29%)
  Pallas kernels  21.5 us (19%)
  local copies, waits for them, and re-layouts  3.56 us (3%)
  other arithmetic  1.79 us (2%)
    all_to_all x2, blocking collectives, exchange(): return lax.all_to_all(x, 'tau', split_axis=0, concat_axis=0, tiled=True)  55.5 us
    ppermute x1, starting transfers between devices, body(): c0 = lax.ppermute(atom0, BOTH, ALONG_Z)  14.1 us
    pallas_call x2, Pallas kernels, apply_z(): pl.pallas_call(functools.partial(z_kernel, slot), in_specs=[SM, VM, VM, V...  12.6 us
    ppermute x1, starting transfers between devices, body(): c1 = lax.ppermute(c1, 'pair', SWAP)  8.24 us
    ppermute x1, starting transfers between devices, body(): other_far = lax.ppermute(far[1:2], 'pair', SWAP)  4.77 us
    ppermute x1, starting transfers between devices, body(): far = lax.ppermute(outgoing, BOTH, ALONG_Z)  3.63 us
    unnamed x20, local copies, waits for them, and re-layouts  3.55 us
    pallas_call x1, Pallas kernels, last_product(): pl.pallas_call(last_kernel, in_specs=[VM] * 5, out_specs=VM, scratch_shap...  3.29 us
  transfers between devices with their start and end apart: 5, of which 0 were waited for; matrix products, arithmetic and copies ran while one was open for 0% of the time, Pallas kernels for 11%

profile of v2, /device:TPU:1, one launch (start us, length us, event | category | flops | bytes accessed | tf_op | source)
XLA Modules:
  0.0 115.9 jit_solution(6627229352003639845)
XLA Ops:
  0.0 1.1 convert_bitcast_fusion.peers_ref
  1.1 0.6 pad_add_fusion.spot_ref
  1.8 3.1 %shard_map.136 = (bf16[32,8,512]{2,1,0:T(8,128)(2,1)}, bf16[1,128,1024]{2,1,0:T(8,128)(2,1)}, bf16[1,128,1024]{2,1,0:T(8,128)(2,1)}, s32[2]{0:T(128)}) custom-call(s32[2]{0:T(128)} %pad_add_fusion.spot_ref, s32[32]{0:T(128)} %partner_ref.3, s32[32]{0:T(128)} %asked_ref.1, s32[32]{0:T(128)} %homes_ref.1, s32[256]{0:T(256)} %constant.28.clone.dst_ref, ...), custom_call_target="tpu_custom_call" | custom-call | flops 200000000 | bytes 3000000 | tf_op jit(solution)/shard_map/pallas_call | solution.py:114
  4.9 14.9 %all_to_all.10 = bf16[32,8,512]{2,1,0:T(8,128)(2,1)S(1)} all-to-all(bf16[32,8,512]{2,1,0:T(8,128)(2,1)} %get-tuple-element.12), channel_id=1, replica_groups=mesh['pair'=32,'tau'=16] {'tau'}, dimensions={0} | all-to-all | bytes 524288 | tf_op jit(solution)/shard_map/all_to_all | solution.py:280
  19.8 3.6 %collective-permute-start.3 = (bf16[2,16,8,256]{3,2,1,0:T(8,128)(2,1)S(1)}, bf16[2,16,8,256]{3,2,1,0:T(8,128)(2,1)S(1)}, u32[]{:S(2)}, u32[]{:S(2)}) collective-permute-start(bf16[2,16,8,256]{3,2,1,0:T(8,128)(2,1)S(1)} %copy_bitcast_fusion), channel_id=1, source_target_pairs={{0,32},{1,225},{2,290},{3,483},{4,68},{5,453},{6,198},{7,327},{8,1... | collective-permute-start | bytes 393224 | tf_op jit(solution)/shard_map/ppermute | solution.py:292
  23.5 14.1 %collective-permute-start = (bf16[1,128,1024]{2,1,0:T(8,128)(2,1)}, bf16[1,128,1024]{2,1,0:T(8,128)(2,1)S(1)}, u32[]{:S(2)}, u32[]{:S(2)}) collective-permute-start(bf16[1,128,1024]{2,1,0:T(8,128)(2,1)} %get-tuple-element.11), channel_id=1, source_target_pairs={{0,32},{1,225},{2,290},{3,483},{4,68},{5,453},{6,198},{7,327},{8,1... | collective-permute-start | bytes 786440 | tf_op jit(solution)/shard_map/ppermute | solution.py:289
  37.6 2.6 %collective-permute-start.1 = (bf16[1,128,1024]{2,1,0:T(8,128)(2,1)}, bf16[1,128,1024]{2,1,0:T(8,128)(2,1)S(1)}, u32[]{:S(2)}, u32[]{:S(2)}) collective-permute-start(bf16[1,128,1024]{2,1,0:T(8,128)(2,1)} %get-tuple-element.14), channel_id=1, source_target_pairs={{0,32},{1,225},{2,290},{3,483},{4,68},{5,453},{6,198},{7,327},{8,1... | collective-permute-start | bytes 786440 | tf_op jit(solution)/shard_map/ppermute | solution.py:294
  40.2 0.0 collective-permute-done.3.far_ref
  40.2 4.8 %collective-permute-start.4 = (bf16[1,16,8,256]{3,2,1,0:T(8,128)(2,1)S(1)}, bf16[1,16,8,256]{3,2,1,0:T(8,128)(2,1)S(1)}, u32[]{:S(2)}, u32[]{:S(2)}) collective-permute-start(bf16[1,16,8,256]{3,2,1,0:T(8,128)(2,1)S(1)} %slice.9), channel_id=1, source_target_pairs={{0,16},{16,0},{32,48},{48,32},{64,80},{80,64},{96,112},{112,96},{1... | collective-permute-start | bytes 196616 | tf_op jit(solution)/shard_map/ppermute | solution.py:293
  45.0 0.0 copy-start
  45.0 1.2 %copy-done = bf16[4,128,1024]{2,1,0:T(8,128)(2,1)S(1)} copy-done((bf16[4,128,1024]{2,1,0:T(8,128)(2,1)S(1)}, bf16[4,128,1024]{2,1,0:T(8,128)(2,1)}, u32[]{:S(2)}) %copy-start) | copy-done | bytes 1048600
  46.3 0.6 copy-done.5
  46.9 0.8 copy-done.6
  47.7 0.8 copy-done.8
  48.6 6.3 %shard_map.137.z0_ref = bf16[16,128,1024]{2,1,0:T(8,128)(2,1)S(1)} custom-call(s32[2]{0:T(128)S(1)} %copy-done.5, bf16[4,128,1024]{2,1,0:T(8,128)(2,1)S(1)} %copy-done, bf16[16,2,8,512]{3,2,1,0:T(8,128)(2,1)S(1)} %bitcast.15, bf16[2,16,8,256]{3,2,1,0:T(8,128)(2,1)S(1)} %collective-permute-done.3.far_ref, bf16[128,256]{1,0:T(8,128)(2,1)S(1)} %copy-done.8, ...), custom_call_target="tpu_custom_call" | custom-call | flops 8000000000 | bytes 5000000 | tf_op jit(solution)/shard_map/pallas_call | solution.py:200
  54.9 0.0 copy-start.1
  54.9 0.0 collective-permute-done.1
  54.9 8.2 %collective-permute-start.2 = (bf16[1,128,1024]{2,1,0:T(8,128)(2,1)S(1)}, bf16[1,128,1024]{2,1,0:T(8,128)(2,1)S(1)}, u32[]{:S(2)}, u32[]{:S(2)}) collective-permute-start(bf16[1,128,1024]{2,1,0:T(8,128)(2,1)S(1)} %collective-permute-done.1), channel_id=1, source_target_pairs={{0,16},{16,0},{32,48},{48,32},{64,80},{80,64},{96,112},{112,96},{1... | collective-permute-start | bytes 786440 | tf_op jit(solution)/shard_map/ppermute | solution.py:295
  63.1 0.0 collective-permute-done.4.far_ref
  63.2 0.0 copy-done.7
  63.2 0.0 copy-done.9
  63.2 6.3 %shard_map.138.z1_ref = bf16[16,128,1024]{2,1,0:T(8,128)(2,1)S(1)} custom-call(s32[2]{0:T(128)S(1)} %copy-done.5, bf16[4,128,1024]{2,1,0:T(8,128)(2,1)S(1)} %copy-done, bf16[16,2,8,512]{3,2,1,0:T(8,128)(2,1)S(1)} %bitcast.16, bf16[1,16,8,256]{3,2,1,0:T(8,128)(2,1)S(1)} %collective-permute-done.4.far_ref, bf16[128,256]{1,0:T(8,128)(2,1)S(1)} %copy-done.9, ...), custom_call_target="tpu_custom_call" | custom-call | flops 8000000000 | bytes 5000000 | tf_op jit(solution)/shard_map/pallas_call | solution.py:200
  69.5 0.0 copy-start.2
  69.5 0.0 copy-start.3
  69.5 0.0 copy-start.4
  69.5 0.0 collective-permute-done.c0_ref
  69.5 0.0 collective-permute-done.2.c1_ref
  69.6 0.0 copy-done.1
  69.6 3.3 %shard_map.139 = bf16[16,2,128,128]{3,2,1,0:T(8,128)(2,1)S(1)} custom-call(bf16[1,128,1024]{2,1,0:T(8,128)(2,1)S(1)} %collective-permute-done.c0_ref, bf16[1,128,1024]{2,1,0:T(8,128)(2,1)S(1)} %collective-permute-done.2.c1_ref, bf16[16,128,1024]{2,1,0:T(8,128)(2,1)S(1)} %shard_map.137.z0_ref, bf16[16,128,1024]{2,1,0:T(8,128)(2,1)S(1)} %shard_map.138.z1_ref, ...), custom_call_target="tpu_custom_call" | custom-call | flops 1200000000 | bytes 10000000 | tf_op jit(solution)/shard_map/pallas_call | solution.py:236
  72.9 40.5 %all_to_all.11.in_ref = bf16[32,128,128]{2,1,0:T(8,128)(2,1)S(1)} all-to-all(bf16[32,128,128]{2,1,0:T(8,128)(2,1)S(1)} %bitcast.13), channel_id=1, replica_groups=mesh['pair'=32,'tau'=16] {'tau'}, dimensions={0} | all-to-all | bytes 2097152 | tf_op jit(solution)/shard_map/all_to_all | solution.py:280
  113.4 0.0 copy-done.4
  113.4 2.5 %shard_map.140 = f32[32,128,128]{2,1,0:T(8,128)} custom-call(s32[2]{0:T(128)S(1)} %copy-done.3, s32[32]{0:T(128)S(1)} %copy-done.2, s32[256]{0:T(256)S(1)} %copy-done.4, bf16[32,128,128]{2,1,0:T(8,128)(2,1)S(1)} %all_to_all.11.in_ref), custom_call_target="tpu_custom_call" | custom-call | flops 1000000 | bytes 3000000 | tf_op jit(solution)/shard_map/pallas_call | solution.py:257
  (9 shorter events, 0.0 us)
Async XLA Ops:
  19.8 20.4 %collective-permute-start.3 = (bf16[2,16,8,256]{3,2,1,0:T(8,128)(2,1)S(1)}, bf16[2,16,8,256]{3,2,1,0:T(8,128)(2,1)S(1)}, u32[]{:S(2)}, u32[]{:S(2)}) collective-permute-start(bf16[2,16,8,256]{3,2,1,0:T(8,128)(2,1)S(1)} %copy_bitcast_fusion), channel_id=1, source_target_pairs={{0,32},{1,225},{2,290},{3,483},{4,68},{5,453},{6,198},{7,327},{8,1... | collective-permute-start | bytes 393224 | tf_op jit(solution)/shard_map/ppermute | solution.py:292
  23.5 46.1 %collective-permute-start = (bf16[1,128,1024]{2,1,0:T(8,128)(2,1)}, bf16[1,128,1024]{2,1,0:T(8,128)(2,1)S(1)}, u32[]{:S(2)}, u32[]{:S(2)}) collective-permute-start(bf16[1,128,1024]{2,1,0:T(8,128)(2,1)} %get-tuple-element.11), channel_id=1, source_target_pairs={{0,32},{1,225},{2,290},{3,483},{4,68},{5,453},{6,198},{7,327},{8,1... | collective-permute-start | bytes 786440 | tf_op jit(solution)/shard_map/ppermute | solution.py:289
  37.6 17.3 %collective-permute-start.1 = (bf16[1,128,1024]{2,1,0:T(8,128)(2,1)}, bf16[1,128,1024]{2,1,0:T(8,128)(2,1)S(1)}, u32[]{:S(2)}, u32[]{:S(2)}) collective-permute-start(bf16[1,128,1024]{2,1,0:T(8,128)(2,1)} %get-tuple-element.14), channel_id=1, source_target_pairs={{0,32},{1,225},{2,290},{3,483},{4,68},{5,453},{6,198},{7,327},{8,1... | collective-permute-start | bytes 786440 | tf_op jit(solution)/shard_map/ppermute | solution.py:294
  40.2 22.9 %collective-permute-start.4 = (bf16[1,16,8,256]{3,2,1,0:T(8,128)(2,1)S(1)}, bf16[1,16,8,256]{3,2,1,0:T(8,128)(2,1)S(1)}, u32[]{:S(2)}, u32[]{:S(2)}) collective-permute-start(bf16[1,16,8,256]{3,2,1,0:T(8,128)(2,1)S(1)} %slice.9), channel_id=1, source_target_pairs={{0,16},{16,0},{32,48},{48,32},{64,80},{80,64},{96,112},{112,96},{1... | collective-permute-start | bytes 196616 | tf_op jit(solution)/shard_map/ppermute | solution.py:293
  45.0 1.2 %copy-start = (bf16[4,128,1024]{2,1,0:T(8,128)(2,1)S(1)}, bf16[4,128,1024]{2,1,0:T(8,128)(2,1)}, u32[]{:S(2)}) copy-start(bf16[4,128,1024]{2,1,0:T(8,128)(2,1)} %ci_ref.3) | copy-start | bytes 3145732
  46.2 0.6 copy-start.5
  46.9 0.8 copy-start.6
  47.7 0.8 copy-start.8
  48.5 14.6 %copy-start.7 = (bf16[128,256]{1,0:T(8,128)(2,1)S(1)}, bf16[128,256]{1,0:T(8,128)(2,1)}, u32[]{:S(2)}) copy-start(bf16[128,256]{1,0:T(8,128)(2,1)} %constant.26.clone.eh_ref) | copy-start | bytes 196612
  48.6 14.6 %copy-start.9 = (bf16[128,256]{1,0:T(8,128)(2,1)S(1)}, bf16[128,256]{1,0:T(8,128)(2,1)}, u32[]{:S(2)}) copy-start(bf16[128,256]{1,0:T(8,128)(2,1)} %constant.25.clone.eg_ref) | copy-start | bytes 196612
  54.9 14.7 %copy-start.1 = (bf16[256,256]{1,0:T(8,128)(2,1)S(1)}, bf16[256,256]{1,0:T(8,128)(2,1)}, u32[]{:S(2)}) copy-start(bf16[256,256]{1,0:T(8,128)(2,1)} %constant.27.clone.pm_ref) | copy-start | bytes 393220
  54.9 14.7 %collective-permute-start.2 = (bf16[1,128,1024]{2,1,0:T(8,128)(2,1)S(1)}, bf16[1,128,1024]{2,1,0:T(8,128)(2,1)S(1)}, u32[]{:S(2)}, u32[]{:S(2)}) collective-permute-start(bf16[1,128,1024]{2,1,0:T(8,128)(2,1)S(1)} %collective-permute-done.1), channel_id=1, source_target_pairs={{0,16},{16,0},{32,48},{48,32},{64,80},{80,64},{96,112},{112,96},{1... | collective-permute-start | bytes 786440 | tf_op jit(solution)/shard_map/ppermute | solution.py:295
  69.5 43.9 %copy-start.2 = (s32[32]{0:T(128)S(1)}, s32[32]{0:T(128)}, u32[]{:S(2)}) copy-start(s32[32]{0:T(128)} %partner_ref.3) | copy-start | bytes 388
  69.5 43.9 %copy-start.3 = (s32[2]{0:T(128)S(1)}, s32[2]{0:T(128)}, u32[]{:S(2)}) copy-start(s32[2]{0:T(128)} %pad_add_fusion.spot_ref) | copy-start | bytes 28
  69.5 43.9 %copy-start.4 = (s32[256]{0:T(256)S(1)}, s32[256]{0:T(256)}, u32[]{:S(2)}) copy-start(s32[256]{0:T(256)} %constant.32.clone.column_ref) | copy-start | bytes 3076

commit v3 on v2

--- a/solution.py
+++ b/solution.py
@@ -59,22 +59,18 @@
 
 
 def prepare_kernel(
-    spot_ref, partner_ref, asked_ref, homes_ref, dst_ref, src_ref, near_ref, away_ref, peers_ref, coeff_ref, gf_ref,
-    gb_ref, send_ref, atom0_ref, atom1_ref, home_ref, wide
+    asked_ref, dst_ref, near_ref, away_ref, peers_ref, coeff_ref, gf_ref, gb_ref, send_ref, atom0_ref, atom1a_ref,
+    atom1b_ref, wide
 ):
-    p, k = spot_ref[0], spot_ref[1]
+    p, k = lax.axis_index("pair"), lax.axis_index("tau")
     z, core = p // 2, p % 2
     to = 2 * dst_ref[z * N_TAU + k]
-    come = 2 * src_ref[z * N_TAU + k]
-    for j, atom_ref in enumerate((atom0_ref, atom1_ref)):
-        side = core if j == 0 else 1 - core
-        atom_ref[0] = coeff_ref[asked_ref[to + side]]
-        found = jnp.int32(0)
-        for m in range(N_PAIR):
-            found = jnp.where(partner_ref[m] == come + side, homes_ref[m], found)
-        home_ref[j] = found
+    atom0_ref[0] = coeff_ref[asked_ref[to + core]]
+    other = asked_ref[to + 1 - core]
+    atom1a_ref[0] = coeff_ref[other, :64]
+    atom1b_ref[0] = coeff_ref[other, 64:]
     eye = lax.broadcasted_iota(jnp.int32, (32, 32), 0) == lax.broadcasted_iota(jnp.int32, (32, 32), 1)
-    peers = peers_ref[...]
+    peers = peers_ref[...].astype(F32)
 
     def pick(table_ref):
         row = table_ref[pl.ds(p, 1), :]
@@ -103,7 +99,7 @@
     send_ref[...] = wide[...].astype(BF16)
 
 
-def prepare(spot, partner, send_atoms, home_atom, coeff, fwd, bwd):
+def prepare(partner, send_atoms, coeff, fwd, bwd):
     sides = np.arange(N_PAIR) % 2
     near = np.zeros((N_PAIR, N_PAIR), np.float32)
     away = np.zeros((N_PAIR, N_PAIR), np.float32)
@@ -113,38 +109,58 @@
             away[p, j::2] = 2 * DST[p // 2] + (sides[p] ^ j)
     return pl.pallas_call(
         prepare_kernel,
-        in_specs=[SM] * 6 + [VM] * 6,
-        out_specs=[VM, VM, VM, SM],
+        in_specs=[SM] * 2 + [VM] * 6,
+        out_specs=[VM] * 4,
         scratch_shapes=[pltpu.VMEM((32, 8, 512), F32)],
         out_shape=[
             jax.ShapeDtypeStruct((32, 8, 512), BF16),
             jax.ShapeDtypeStruct((1, AUX, 1024), BF16),
-            jax.ShapeDtypeStruct((1, AUX, 1024), BF16),
-            jax.ShapeDtypeStruct((2,), jnp.int32),
+            jax.ShapeDtypeStruct((1, 64, 1024), BF16),
+            jax.ShapeDtypeStruct((1, 64, 1024), BF16),
         ],
         cost_estimate=pl.CostEstimate(flops=200_000_000, bytes_accessed=3_000_000, transcendentals=0),
     )(
-        spot,
-        partner,
         send_atoms,
-        home_atom,
         jnp.asarray(DST.reshape(-1)),
-        jnp.asarray(SRC.reshape(-1)),
         jnp.asarray(near),
         jnp.asarray(away),
-        partner.astype(F32).reshape(1, N_PAIR),
+        partner.reshape(1, N_PAIR),
         coeff,
         fwd,
         bwd,
     )
 
 
+def turn_kernel(partner_ref, homes_ref, src_ref, coeff_ref, cin_ref):
+    p, k = lax.axis_index("pair"), lax.axis_index("tau")
+    come = 2 * src_ref[(p // 2) * N_TAU + k]
+    for j in range(2):
+        side = (p + j) % 2
+        home = jnp.int32(0)
+        for m in range(N_PAIR):
+            home = jnp.where(partner_ref[m] == come + side, homes_ref[m], home)
+        for c in range(4):
+            cin_ref[j, :, c * 128:(c + 1) * 128] = coeff_ref[home, :, c * 256:(c + 1) * 256].astype(F32).T.astype(BF16)
+
+
+def turn_home(partner, home_atom, coeff):
+    return pl.pallas_call(
+        turn_kernel,
+        in_specs=[SM] * 3 + [VM],
+        out_specs=VM,
+        out_shape=jax.ShapeDtypeStruct((2, 256, 512), BF16),
+        cost_estimate=pl.CostEstimate(flops=100_000_000, bytes_accessed=2_000_000, transcendentals=0),
+    )(partner, home_atom, jnp.asarray(SRC.reshape(-1)), coeff)
+
+
 UNROLL = 8
 
 
-def z_kernel(slot, home_ref, ci_ref, own_ref, far_ref, eg_ref, eh_ref, z_ref, cin, fb, bb, s_a, s_b):
-    for c in range(4):
-        cin[:, c * 128:(c + 1) * 128] = ci_ref[home_ref[slot], :, c * 256:(c + 1) * 256].astype(F32).T.astype(BF16)
+def z_kernel(slot, cin_ref, own_ref, far_ref, z_ref, fb, bb, s_a, s_b):
+    i = lax.broadcasted_iota(jnp.int32, (128, 256), 0) % 32
+    j = lax.broadcasted_iota(jnp.int32, (128, 256), 1)
+    eg = jnp.where(i == j // 8, 1.0, 0.0).astype(BF16)
+    eh = jnp.where(i == j % 32, 1.0, 0.0).astype(BF16)
     keep = (lax.broadcasted_iota(jnp.int32, (64, 128), 0) // 16) == (lax.broadcasted_iota(jnp.int32, (64, 128), 1) // 32)
 
     def unpack(packed, e, dst, kind):
@@ -152,10 +168,10 @@
         rep = jnp.where(keep[None], rep, 0.0).reshape(N_TAU * 64, 128).astype(BF16)
         dst[:, kind] = dot(rep, e).astype(BF16).reshape(N_TAU, 64, 256)
 
-    unpack(own_ref[:, slot, :, 0:128], eh_ref[...], fb, 0)
-    unpack(far_ref[0, :, :, 0:128], eh_ref[...], fb, 1)
-    unpack(own_ref[:, slot, :, 128:256], eg_ref[...], bb, 0)
-    unpack(far_ref[0, :, :, 128:256], eg_ref[...], bb, 1)
+    unpack(own_ref[:, slot, :, 0:128], eh, fb, 0)
+    unpack(far_ref[0, :, :, 0:128], eh, fb, 1)
+    unpack(own_ref[:, slot, :, 128:256], eg, bb, 0)
+    unpack(far_ref[0, :, :, 128:256], eg, bb, 1)
     row = lax.broadcasted_iota(jnp.int32, (64, 256), 0) // 8
     lane = lax.broadcasted_iota(jnp.int32, (64, 256), 1)
     mask_minor = jnp.where(row == lane // 32, 1.0, 0.0).astype(BF16)
@@ -168,7 +184,7 @@
 
     def first(t, buf):
         for kind in range(2):
-            s1 = dot(spread(fb[t, kind], mask_minor), cin[...]).astype(BF16)
+            s1 = dot(spread(fb[t, kind], mask_minor), cin_ref[slot]).astype(BF16)
             for h in range(4):
                 for a in range(4):
                     buf[kind * 256 + a * 64:kind * 256 + (a + 1) * 64, h * 128:(h + 1) * 128] = s1[
@@ -196,23 +212,26 @@
     lax.fori_loop(0, N_TAU // UNROLL, step, 0)
 
 
-def apply_z(slot, home, coeff, own, far, eg, eh):
+def apply_z(slot, cin, own, far):
     return pl.pallas_call(
         functools.partial(z_kernel, slot),
-        in_specs=[SM, VM, VM, VM, VM, VM],
+        in_specs=[VM] * 3,
         out_specs=VM,
-        scratch_shapes=[pltpu.VMEM((256, 512), BF16)]
-        + [pltpu.VMEM((N_TAU, 2, 64, 256), BF16)] * 2
+        scratch_shapes=[pltpu.VMEM((N_TAU, 2, 64, 256), BF16)] * 2
         + [pltpu.VMEM((512, 512), BF16)] * 2,
         out_shape=jax.ShapeDtypeStruct((N_TAU, AUX, 1024), BF16),
         compiler_params=pltpu.CompilerParams(vmem_limit_bytes=16 * 2**20),
         cost_estimate=pl.CostEstimate(flops=8_000_000_000, bytes_accessed=5_000_000, transcendentals=0),
-    )(home, coeff, own, far, eg, eh)
-
-
-def last_kernel(c0_ref, c1_ref, z0_ref, z1_ref, pm_ref, out_ref, cp):
-    for j, ref in enumerate((c0_ref, c1_ref)):
-        turned = [dot(ref[0, :, a * 256:(a + 1) * 256], pm_ref[...]) for a in range(4)]
+    )(cin, own, far)
+
+
+def last_kernel(c0_ref, c1a_ref, c1b_ref, z0_ref, z1_ref, out_ref, cp):
+    r = lax.broadcasted_iota(jnp.int32, (256, 256), 0)
+    q = lax.broadcasted_iota(jnp.int32, (256, 256), 1)
+    pm = jnp.where(q == (r % 32 // 8) * 64 + (r % 8) * 8 + r // 32, 1.0, 0.0).astype(BF16)
+    for j in range(2):
+        atom = c0_ref[0] if j == 0 else jnp.concatenate([c1a_ref[0], c1b_ref[0]], axis=0)
+        turned = [dot(atom[:, a * 256:(a + 1) * 256], pm) for a in range(4)]
         for h in range(4):
             cp[j, :, h * 256:(h + 1) * 256] = jnp.concatenate(
                 [turned[a][:, h * 64:(h + 1) * 64] for a in range(4)], axis=1
@@ -232,7 +251,7 @@
     lax.fori_loop(0, N_TAU // 4, step, 0)
 
 
-def last_product(c0, c1, z0, z1, pm):
+def last_product(c0, c1a, c1b, z0, z1):
     return pl.pallas_call(
         last_kernel,
         in_specs=[VM] * 5,
@@ -241,63 +260,56 @@
         out_shape=jax.ShapeDtypeStruct((N_TAU, 2, AUX, AUX), BF16),
         compiler_params=pltpu.CompilerParams(vmem_limit_bytes=16 * 2**20),
         cost_estimate=pl.CostEstimate(flops=1_200_000_000, bytes_accessed=10_000_000, transcendentals=0),
-    )(c0, c1, z0, z1, pm)
-
-
-def finish_kernel(spot_ref, partner_ref, column_ref, in_ref, out_ref):
+    )(c0, c1a, c1b, z0, z1)
+
+
+def finish_kernel(partner_ref, column_ref, in_ref, out_ref):
     base = pl.program_id(0) * 8
-    p = spot_ref[0]
+    p = lax.axis_index("pair")
     for i in range(8):
         other = partner_ref[base + i]
         place = 2 * column_ref[(p // 2) * CHIPS + other // 2] + (p + other) % 2
         out_ref[i] = in_ref[place].astype(F32)
 
 
-def finish(spot, partner, tiles):
+def finish(partner, tiles):
     return pl.pallas_call(
         finish_kernel,
         grid=(4,),
-        in_specs=[SM, SM, SM, VM],
+        in_specs=[SM, SM, VM],
         out_specs=pl.BlockSpec((8, AUX, AUX), lambda i: (i, 0, 0)),
         out_shape=jax.ShapeDtypeStruct((32, AUX, AUX), F32),
         compiler_params=pltpu.CompilerParams(vmem_limit_bytes=8 * 2**20),
         cost_estimate=pl.CostEstimate(flops=1_000_000, bytes_accessed=3_000_000, transcendentals=0),
-    )(spot, partner, jnp.asarray(COLUMN.reshape(-1)), tiles)
-
-
-def constants():
-    i = np.arange(128)[:, None]
-    j = np.arange(256)[None, :]
-    eg = ((i % 32) == (j // 8)).astype(np.float32)
-    eh = ((i % 32) == (j % 32)).astype(np.float32)
-    r = np.arange(256)[:, None]
-    lo, b = r // 32, r % 32
-    pm = (j == (b // 8) * 64 + (b % 8) * 8 + lo).astype(np.float32)
-    return jnp.asarray(eg, BF16), jnp.asarray(eh, BF16), jnp.asarray(pm, BF16)
+    )(partner, jnp.asarray(COLUMN.reshape(-1)), tiles)
 
 
 def exchange(x):
     return lax.all_to_all(x, "tau", split_axis=0, concat_axis=0, tiled=True)
 
 
+def send_z(x):
+    return lax.ppermute(x, BOTH, ALONG_Z)
+
+
+def swap(x):
+    return lax.ppermute(x, "pair", SWAP)
+
+
 def body(coeff, green_fwd, green_bwd, home_atom, send_atoms, partner, mirror):
-    spot = jnp.stack([lax.axis_index("pair"), lax.axis_index("tau")]).astype(jnp.int32)
-    eg, eh, pm = constants()
-    send, atom0, atom1, home = prepare(
-        spot, partner, send_atoms, home_atom, coeff, green_fwd[:, 0, :], green_bwd[:, 0, :]
-    )
-    c0 = lax.ppermute(atom0, BOTH, ALONG_Z)
+    send, atom0, atom1a, atom1b = prepare(partner, send_atoms, coeff, green_fwd[:, 0, :], green_bwd[:, 0, :])
     greens = exchange(send).reshape(N_TAU, 2, 8, 512)
-    outgoing, atom1 = lax.optimization_barrier((greens[:, :, :, 256:512].transpose(1, 0, 2, 3), atom1))
-    far = lax.ppermute(outgoing, BOTH, ALONG_Z)
-    other_far = lax.ppermute(far[1:2], "pair", SWAP)
-    c1 = lax.ppermute(atom1, BOTH, ALONG_Z)
-    c1 = lax.ppermute(c1, "pair", SWAP)
-    z0 = apply_z(0, home, coeff, greens, far, eg, eh)
-    z1 = apply_z(1, home, coeff, greens, other_far, eg, eh)
-    tiles = last_product(c0, c1, z0, z1, pm)
+    c1a = send_z(atom1a)
+    cin = turn_home(partner, home_atom, coeff)
+    outgoing, atom0, atom1b = lax.optimization_barrier((greens[:, :, :, 256:512].transpose(1, 0, 2, 3), atom0, atom1b))
+    far = send_z(outgoing)
+    c1b = send_z(atom1b)
+    c0 = send_z(atom0)
+    z0 = apply_z(0, cin, greens, far)
+    z1 = apply_z(1, cin, greens, swap(far[1:2]))
+    tiles = last_product(c0, swap(c1a), swap(c1b), z0, z1)
     back = exchange(tiles.reshape(32, AUX, AUX))
-    return finish(spot, partner, back).reshape(32, 1, AUX, AUX)
+    return finish(partner, back).reshape(32, 1, AUX, AUX)
 
 
 def solution(mesh):

time: 116 us -> 103 us (0.89)
  the two profiles are of different devices: /device:TPU:1 before, /device:TPU:64 now
where the time goes in v3:
time: 103 us; the launch traced here: 102 us
  starting transfers between devices  40.1 us (39%)
  blocking collectives  38.4 us (37%)
  Pallas kernels  22.7 us (22%)
  local copies, waits for them, and re-layouts  1.07 us (1%)
    all_to_all x1, blocking collectives, exchange(): return lax.all_to_all(x, 'tau', split_axis=0, concat_axis=0, tiled=True)  38.4 us
    ppermute x4, starting transfers between devices, send_z(): return lax.ppermute(x, BOTH, ALONG_Z)  26.8 us
    pallas_call x2, Pallas kernels, apply_z(): pl.pallas_call(functools.partial(z_kernel, slot), in_specs=[VM] * 3, out_...  11.6 us
    all_to_all x1, starting transfers between devices, exchange(): return lax.all_to_all(x, 'tau', split_axis=0, concat_axis=0, tiled=True)  7.04 us
    ppermute x3, starting transfers between devices, swap(): return lax.ppermute(x, 'pair', SWAP)  6.24 us
    pallas_call x1, Pallas kernels, last_product(): pl.pallas_call(last_kernel, in_specs=[VM] * 5, out_specs=VM, scratch_shap...  3.26 us
    pallas_call x1, Pallas kernels, prepare(): pl.pallas_call(prepare_kernel, in_specs=[SM] * 2 + [VM] * 6, out_specs=[V...  3.06 us
    pallas_call x1, Pallas kernels, finish(): pl.pallas_call(finish_kernel, grid=(4,), in_specs=[SM, SM, VM], out_specs...  2.53 us
  transfers between devices with their start and end apart: 8, of which 0 were waited for; matrix products, arithmetic and copies ran while one was open for 0% of the time, Pallas kernels for 14%

profile of v3, /device:TPU:64, one launch (start us, length us, event | category | flops | bytes accessed | tf_op | source)
XLA Modules:
  0.0 102.5 jit_solution(9920689581359823011)
XLA Ops:
  0.0 3.1 %shard_map.109 = (bf16[32,8,512]{2,1,0:T(8,128)(2,1)}, bf16[1,128,1024]{2,1,0:T(8,128)(2,1)}, bf16[1,64,1024]{2,1,0:T(8,128)(2,1)}, bf16[1,64,1024]{2,1,0:T(8,128)(2,1)}) custom-call(s32[32]{0:T(128)} %asked_ref.1, s32[256]{0:T(256)} %constant.10.clone.dst_ref, f32[32,32]{1,0:T(8,128)} %constant.11.clone.near_ref, f32[32,32]{1,0:T(8,128)} %constant.12.clone.away_ref, ...), custom_call_target="tpu_custom_call" | custom-call | flops 200000000 | bytes 3000000 | tf_op jit(solution)/shard_map/pallas_call | solution.py:110
  3.1 7.0 %all-to-all-start = ((bf16[32,8,512]{2,1,0:T(8,128)(2,1)}), bf16[32,8,512]{2,1,0:T(8,128)(2,1)S(1)}, u32[]{:S(2)}, u32[]{:S(2)}) async-start(bf16[32,8,512]{2,1,0:T(8,128)(2,1)} %get-tuple-element.12), calls=%async_computation | async-start | bytes 524288 | tf_op jit(solution)/shard_map/all_to_all | solution.py:288
  10.1 13.5 %collective-permute-start.1 = (bf16[1,64,1024]{2,1,0:T(8,128)(2,1)}, bf16[1,64,1024]{2,1,0:T(8,128)(2,1)S(1)}, u32[]{:S(2)}, u32[]{:S(2)}) collective-permute-start(bf16[1,64,1024]{2,1,0:T(8,128)(2,1)} %get-tuple-element.16), channel_id=1, source_target_pairs={{0,32},{1,225},{2,290},{3,483},{4,68},{5,453},{6,198},{7,327},{8,1... | collective-permute-start | bytes 393224 | tf_op jit(solution)/shard_map/ppermute | solution.py:292
  23.6 0.0 all-to-all-done
  23.6 8.5 %collective-permute-start.5 = (bf16[2,16,8,256]{3,2,1,0:T(8,128)(2,1)S(1)}, bf16[2,16,8,256]{3,2,1,0:T(8,128)(2,1)S(1)}, u32[]{:S(2)}, u32[]{:S(2)}) collective-permute-start(bf16[2,16,8,256]{3,2,1,0:T(8,128)(2,1)S(1)} %copy_bitcast_fusion), channel_id=1, source_target_pairs={{0,32},{1,225},{2,290},{3,483},{4,68},{5,453},{6,198},{7,327},{8,1... | collective-permute-start | bytes 393224 | tf_op jit(solution)/shard_map/ppermute | solution.py:292
  32.1 2.9 %collective-permute-start.3 = (bf16[1,64,1024]{2,1,0:T(8,128)(2,1)}, bf16[1,64,1024]{2,1,0:T(8,128)(2,1)S(1)}, u32[]{:S(2)}, u32[]{:S(2)}) collective-permute-start(bf16[1,64,1024]{2,1,0:T(8,128)(2,1)} %get-tuple-element.17), channel_id=1, source_target_pairs={{0,32},{1,225},{2,290},{3,483},{4,68},{5,453},{6,198},{7,327},{8,1... | collective-permute-start | bytes 393224 | tf_op jit(solution)/shard_map/ppermute | solution.py:292
  35.0 2.3 %shard_map.110.cin_ref = bf16[2,256,512]{2,1,0:T(8,128)(2,1)} custom-call(s32[32]{0:T(128)} %partner_ref.3, s32[32]{0:T(128)} %homes_ref.1, s32[256]{0:T(256)} %constant.13.clone.src_ref, bf16[4,128,1024]{2,1,0:T(8,128)(2,1)} %coeff_ref.3), custom_call_target="tpu_custom_call" | custom-call | flops 100000000 | bytes 2000000 | tf_op jit(solution)/shard_map/pallas_call | solution.py:147
  37.4 0.0 collective-permute-done.1
  37.4 1.9 %collective-permute-start.2 = (bf16[1,64,1024]{2,1,0:T(8,128)(2,1)S(1)}, bf16[1,64,1024]{2,1,0:T(8,128)(2,1)S(1)}, u32[]{:S(2)}, u32[]{:S(2)}) collective-permute-start(bf16[1,64,1024]{2,1,0:T(8,128)(2,1)S(1)} %collective-permute-done.1), channel_id=1, source_target_pairs={{0,16},{16,0},{32,48},{48,32},{64,80},{80,64},{96,112},{112,96},{1... | collective-permute-start | bytes 393224 | tf_op jit(solution)/shard_map/ppermute | solution.py:296
  39.3 1.9 %collective-permute-start = (bf16[1,128,1024]{2,1,0:T(8,128)(2,1)}, bf16[1,128,1024]{2,1,0:T(8,128)(2,1)S(1)}, u32[]{:S(2)}, u32[]{:S(2)}) collective-permute-start(bf16[1,128,1024]{2,1,0:T(8,128)(2,1)} %get-tuple-element.15), channel_id=1, source_target_pairs={{0,32},{1,225},{2,290},{3,483},{4,68},{5,453},{6,198},{7,327},{8,1... | collective-permute-start | bytes 786440 | tf_op jit(solution)/shard_map/ppermute | solution.py:292
  41.2 0.0 collective-permute-done.5.far_ref
  41.2 2.4 %collective-permute-start.6 = (bf16[1,16,8,256]{3,2,1,0:T(8,128)(2,1)S(1)}, bf16[1,16,8,256]{3,2,1,0:T(8,128)(2,1)S(1)}, u32[]{:S(2)}, u32[]{:S(2)}) collective-permute-start(bf16[1,16,8,256]{3,2,1,0:T(8,128)(2,1)S(1)} %slice.9), channel_id=1, source_target_pairs={{0,16},{16,0},{32,48},{48,32},{64,80},{80,64},{96,112},{112,96},{1... | collective-permute-start | bytes 196616 | tf_op jit(solution)/shard_map/ppermute | solution.py:296
  43.7 0.0 collective-permute-done.3
  43.7 1.9 %collective-permute-start.4 = (bf16[1,64,1024]{2,1,0:T(8,128)(2,1)S(1)}, bf16[1,64,1024]{2,1,0:T(8,128)(2,1)S(1)}, u32[]{:S(2)}, u32[]{:S(2)}) collective-permute-start(bf16[1,64,1024]{2,1,0:T(8,128)(2,1)S(1)} %collective-permute-done.3), channel_id=1, source_target_pairs={{0,16},{16,0},{32,48},{48,32},{64,80},{80,64},{96,112},{112,96},{1... | collective-permute-start | bytes 393224 | tf_op jit(solution)/shard_map/ppermute | solution.py:296
  45.6 0.0 copy-start
  45.6 1.0 %copy-done = bf16[2,256,512]{2,1,0:T(8,128)(2,1)S(1)} copy-done((bf16[2,256,512]{2,1,0:T(8,128)(2,1)S(1)}, bf16[2,256,512]{2,1,0:T(8,128)(2,1)}, u32[]{:S(2)}) %copy-start) | copy-done | bytes 524312
  46.6 5.8 %shard_map.111.z0_ref = bf16[16,128,1024]{2,1,0:T(8,128)(2,1)S(1)} custom-call(bf16[2,256,512]{2,1,0:T(8,128)(2,1)S(1)} %copy-done, bf16[16,2,8,512]{3,2,1,0:T(8,128)(2,1)S(1)} %bitcast.12, bf16[2,16,8,256]{3,2,1,0:T(8,128)(2,1)S(1)} %collective-permute-done.5.far_ref), custom_call_target="tpu_custom_call" | custom-call | flops 8000000000 | bytes 5000000 | tf_op jit(solution)/shard_map/pallas_call | solution.py:216
  52.4 0.0 collective-permute-done.6.far_ref
  52.4 5.8 %shard_map.112.z1_ref = bf16[16,128,1024]{2,1,0:T(8,128)(2,1)S(1)} custom-call(bf16[2,256,512]{2,1,0:T(8,128)(2,1)S(1)} %copy-done, bf16[16,2,8,512]{3,2,1,0:T(8,128)(2,1)S(1)} %bitcast.13, bf16[1,16,8,256]{3,2,1,0:T(8,128)(2,1)S(1)} %collective-permute-done.6.far_ref), custom_call_target="tpu_custom_call" | custom-call | flops 8000000000 | bytes 5000000 | tf_op jit(solution)/shard_map/pallas_call | solution.py:216
  58.2 0.0 copy-start.1
  58.2 0.0 copy-start.2
  58.2 0.0 collective-permute-done.2.c1a_ref
  58.3 0.0 collective-permute-done.4.c1b_ref
  58.3 0.0 collective-permute-done.c0_ref
  58.3 3.3 %shard_map.113 = bf16[16,2,128,128]{3,2,1,0:T(8,128)(2,1)S(1)} custom-call(bf16[1,128,1024]{2,1,0:T(8,128)(2,1)S(1)} %collective-permute-done.c0_ref, bf16[1,64,1024]{2,1,0:T(8,128)(2,1)S(1)} %collective-permute-done.2.c1a_ref, bf16[1,64,1024]{2,1,0:T(8,128)(2,1)S(1)} %collective-permute-done.4.c1b_ref, bf16[16,128,1024]{2,1,0:T(8,128)(2,1)S(1)} %shard_map.111.z0_ref, ...), custom_call_target="tpu_custom_call" | custom-call | flops 1200000000 | bytes 10000000 | tf_op jit(solution)/shard_map/pallas_call | solution.py:255
  61.5 38.4 %all_to_all.10.in_ref = bf16[32,128,128]{2,1,0:T(8,128)(2,1)S(1)} all-to-all(bf16[32,128,128]{2,1,0:T(8,128)(2,1)S(1)} %bitcast.10), channel_id=1, replica_groups=mesh['pair'=32,'tau'=16] {'tau'}, dimensions={0} | all-to-all | bytes 2097152 | tf_op jit(solution)/shard_map/all_to_all | solution.py:288
  99.9 0.0 copy-done.1
  99.9 0.0 copy-done.2
  99.9 2.5 %shard_map.114 = f32[32,128,128]{2,1,0:T(8,128)} custom-call(s32[32]{0:T(128)S(1)} %copy-done.1, s32[256]{0:T(256)S(1)} %copy-done.2, bf16[32,128,128]{2,1,0:T(8,128)(2,1)S(1)} %all_to_all.10.in_ref), custom_call_target="tpu_custom_call" | custom-call | flops 1000000 | bytes 3000000 | tf_op jit(solution)/shard_map/pallas_call | solution.py:276
  (2 shorter events, 0.0 us)
Async XLA Ops:
  3.1 20.5 %all-to-all-start = ((bf16[32,8,512]{2,1,0:T(8,128)(2,1)}), bf16[32,8,512]{2,1,0:T(8,128)(2,1)S(1)}, u32[]{:S(2)}, u32[]{:S(2)}) async-start(bf16[32,8,512]{2,1,0:T(8,128)(2,1)} %get-tuple-element.12), calls=%async_computation | async-start | bytes 524288 | tf_op jit(solution)/shard_map/all_to_all | solution.py:288
  10.1 27.3 %collective-permute-start.1 = (bf16[1,64,1024]{2,1,0:T(8,128)(2,1)}, bf16[1,64,1024]{2,1,0:T(8,128)(2,1)S(1)}, u32[]{:S(2)}, u32[]{:S(2)}) collective-permute-start(bf16[1,64,1024]{2,1,0:T(8,128)(2,1)} %get-tuple-element.16), channel_id=1, source_target_pairs={{0,32},{1,225},{2,290},{3,483},{4,68},{5,453},{6,198},{7,327},{8,1... | collective-permute-start | bytes 393224 | tf_op jit(solution)/shard_map/ppermute | solution.py:292
  23.6 17.6 %collective-permute-start.5 = (bf16[2,16,8,256]{3,2,1,0:T(8,128)(2,1)S(1)}, bf16[2,16,8,256]{3,2,1,0:T(8,128)(2,1)S(1)}, u32[]{:S(2)}, u32[]{:S(2)}) collective-permute-start(bf16[2,16,8,256]{3,2,1,0:T(8,128)(2,1)S(1)} %copy_bitcast_fusion), channel_id=1, source_target_pairs={{0,32},{1,225},{2,290},{3,483},{4,68},{5,453},{6,198},{7,327},{8,1... | collective-permute-start | bytes 393224 | tf_op jit(solution)/shard_map/ppermute | solution.py:292
  32.1 11.5 %collective-permute-start.3 = (bf16[1,64,1024]{2,1,0:T(8,128)(2,1)}, bf16[1,64,1024]{2,1,0:T(8,128)(2,1)S(1)}, u32[]{:S(2)}, u32[]{:S(2)}) collective-permute-start(bf16[1,64,1024]{2,1,0:T(8,128)(2,1)} %get-tuple-element.17), channel_id=1, source_target_pairs={{0,32},{1,225},{2,290},{3,483},{4,68},{5,453},{6,198},{7,327},{8,1... | collective-permute-start | bytes 393224 | tf_op jit(solution)/shard_map/ppermute | solution.py:292
  37.4 20.9 %collective-permute-start.2 = (bf16[1,64,1024]{2,1,0:T(8,128)(2,1)S(1)}, bf16[1,64,1024]{2,1,0:T(8,128)(2,1)S(1)}, u32[]{:S(2)}, u32[]{:S(2)}) collective-permute-start(bf16[1,64,1024]{2,1,0:T(8,128)(2,1)S(1)} %collective-permute-done.1), channel_id=1, source_target_pairs={{0,16},{16,0},{32,48},{48,32},{64,80},{80,64},{96,112},{112,96},{1... | collective-permute-start | bytes 393224 | tf_op jit(solution)/shard_map/ppermute | solution.py:296
  39.3 19.0 %collective-permute-start = (bf16[1,128,1024]{2,1,0:T(8,128)(2,1)}, bf16[1,128,1024]{2,1,0:T(8,128)(2,1)S(1)}, u32[]{:S(2)}, u32[]{:S(2)}) collective-permute-start(bf16[1,128,1024]{2,1,0:T(8,128)(2,1)} %get-tuple-element.15), channel_id=1, source_target_pairs={{0,32},{1,225},{2,290},{3,483},{4,68},{5,453},{6,198},{7,327},{8,1... | collective-permute-start | bytes 786440 | tf_op jit(solution)/shard_map/ppermute | solution.py:292
  41.2 11.2 %collective-permute-start.6 = (bf16[1,16,8,256]{3,2,1,0:T(8,128)(2,1)S(1)}, bf16[1,16,8,256]{3,2,1,0:T(8,128)(2,1)S(1)}, u32[]{:S(2)}, u32[]{:S(2)}) collective-permute-start(bf16[1,16,8,256]{3,2,1,0:T(8,128)(2,1)S(1)} %slice.9), channel_id=1, source_target_pairs={{0,16},{16,0},{32,48},{48,32},{64,80},{80,64},{96,112},{112,96},{1... | collective-permute-start | bytes 196616 | tf_op jit(solution)/shard_map/ppermute | solution.py:296
  43.7 14.6 %collective-permute-start.4 = (bf16[1,64,1024]{2,1,0:T(8,128)(2,1)S(1)}, bf16[1,64,1024]{2,1,0:T(8,128)(2,1)S(1)}, u32[]{:S(2)}, u32[]{:S(2)}) collective-permute-start(bf16[1,64,1024]{2,1,0:T(8,128)(2,1)S(1)} %collective-permute-done.3), channel_id=1, source_target_pairs={{0,16},{16,0},{32,48},{48,32},{64,80},{80,64},{96,112},{112,96},{1... | collective-permute-start | bytes 393224 | tf_op jit(solution)/shard_map/ppermute | solution.py:296
  45.6 1.0 %copy-start = (bf16[2,256,512]{2,1,0:T(8,128)(2,1)S(1)}, bf16[2,256,512]{2,1,0:T(8,128)(2,1)}, u32[]{:S(2)}) copy-start(bf16[2,256,512]{2,1,0:T(8,128)(2,1)} %shard_map.110.cin_ref) | copy-start | bytes 1572868
  58.2 41.7 %copy-start.1 = (s32[32]{0:T(128)S(1)}, s32[32]{0:T(128)}, u32[]{:S(2)}) copy-start(s32[32]{0:T(128)} %partner_ref.3) | copy-start | bytes 388
  58.2 41.7 %copy-start.2 = (s32[256]{0:T(256)S(1)}, s32[256]{0:T(256)}, u32[]{:S(2)}) copy-start(s32[256]{0:T(256)} %constant.14.clone.column_ref) | copy-start | bytes 3076

commit v4 on v3

--- a/solution.py
+++ b/solution.py
@@ -59,16 +59,14 @@
 
 
 def prepare_kernel(
-    asked_ref, dst_ref, near_ref, away_ref, peers_ref, coeff_ref, gf_ref, gb_ref, send_ref, atom0_ref, atom1a_ref,
-    atom1b_ref, wide
+    asked_ref, dst_ref, near_ref, away_ref, peers_ref, coeff_ref, gf_ref, gb_ref, send_ref, atoms_ref,
+    wide
 ):
     p, k = lax.axis_index("pair"), lax.axis_index("tau")
     z, core = p // 2, p % 2
     to = 2 * dst_ref[z * N_TAU + k]
-    atom0_ref[0] = coeff_ref[asked_ref[to + core]]
-    other = asked_ref[to + 1 - core]
-    atom1a_ref[0] = coeff_ref[other, :64]
-    atom1b_ref[0] = coeff_ref[other, 64:]
+    atoms_ref[0] = coeff_ref[asked_ref[to + core]]
+    atoms_ref[1] = coeff_ref[asked_ref[to + 1 - core]]
     eye = lax.broadcasted_iota(jnp.int32, (32, 32), 0) == lax.broadcasted_iota(jnp.int32, (32, 32), 1)
     peers = peers_ref[...].astype(F32)
 
@@ -110,13 +108,11 @@
     return pl.pallas_call(
         prepare_kernel,
         in_specs=[SM] * 2 + [VM] * 6,
-        out_specs=[VM] * 4,
+        out_specs=[VM] * 2,
         scratch_shapes=[pltpu.VMEM((32, 8, 512), F32)],
         out_shape=[
             jax.ShapeDtypeStruct((32, 8, 512), BF16),
-            jax.ShapeDtypeStruct((1, AUX, 1024), BF16),
-            jax.ShapeDtypeStruct((1, 64, 1024), BF16),
-            jax.ShapeDtypeStruct((1, 64, 1024), BF16),
+            jax.ShapeDtypeStruct((2, AUX, 1024), BF16),
         ],
         cost_estimate=pl.CostEstimate(flops=200_000_000, bytes_accessed=3_000_000, transcendentals=0),
     )(
@@ -156,22 +152,19 @@
 UNROLL = 8
 
 
-def z_kernel(slot, cin_ref, own_ref, far_ref, z_ref, fb, bb, s_a, s_b):
+def expand(packed, repeat, dst):
+    rows = packed.shape[0]
     i = lax.broadcasted_iota(jnp.int32, (128, 256), 0) % 32
     j = lax.broadcasted_iota(jnp.int32, (128, 256), 1)
-    eg = jnp.where(i == j // 8, 1.0, 0.0).astype(BF16)
-    eh = jnp.where(i == j % 32, 1.0, 0.0).astype(BF16)
+    e = jnp.where(i == (j // 8 if repeat else j % 32), 1.0, 0.0).astype(BF16)
     keep = (lax.broadcasted_iota(jnp.int32, (64, 128), 0) // 16) == (lax.broadcasted_iota(jnp.int32, (64, 128), 1) // 32)
-
-    def unpack(packed, e, dst, kind):
-        rep = jnp.concatenate([packed.astype(F32)] * 8, axis=1)
-        rep = jnp.where(keep[None], rep, 0.0).reshape(N_TAU * 64, 128).astype(BF16)
-        dst[:, kind] = dot(rep, e).astype(BF16).reshape(N_TAU, 64, 256)
-
-    unpack(own_ref[:, slot, :, 0:128], eh, fb, 0)
-    unpack(far_ref[0, :, :, 0:128], eh, fb, 1)
-    unpack(own_ref[:, slot, :, 128:256], eg, bb, 0)
-    unpack(far_ref[0, :, :, 128:256], eg, bb, 1)
+    rep = jnp.concatenate([packed.astype(F32)] * 8, axis=1)
+    rep = jnp.where(keep[None], rep, 0.0).reshape(rows * 64, 128).astype(BF16)
+    dst[...] = dot(rep, e).astype(BF16).reshape(rows, 64, 256)
+
+
+def pipelined(fb, bb, cin_of, emit, s_a, s_b):
+    count = fb.shape[0]
     row = lax.broadcasted_iota(jnp.int32, (64, 256), 0) // 8
     lane = lax.broadcasted_iota(jnp.int32, (64, 256), 1)
     mask_minor = jnp.where(row == lane // 32, 1.0, 0.0).astype(BF16)
@@ -183,20 +176,15 @@
         )
 
     def first(t, buf):
-        for kind in range(2):
-            s1 = dot(spread(fb[t, kind], mask_minor), cin_ref[slot]).astype(BF16)
-            for h in range(4):
-                for a in range(4):
-                    buf[kind * 256 + a * 64:kind * 256 + (a + 1) * 64, h * 128:(h + 1) * 128] = s1[
-                        h * 64:(h + 1) * 64, a * 128:(a + 1) * 128
-                    ]
+        s1 = dot(spread(fb[t], mask_minor), cin_of(t)).astype(BF16)
+        for h in range(4):
+            for a in range(4):
+                buf[a * 64:(a + 1) * 64, h * 128:(h + 1) * 128] = s1[h * 64:(h + 1) * 64, a * 128:(a + 1) * 128]
 
     def second(t, buf):
-        m2 = jnp.concatenate([spread(bb[t, 0], mask_major), spread(bb[t, 1], mask_major)], axis=1)
+        m2 = spread(bb[t], mask_major)
         for h in range(2):
-            z = dot(m2, buf[:, h * 256:(h + 1) * 256])
-            z_ref[t, :, h * 512:h * 512 + 256] = z[:, :128].T.astype(BF16)
-            z_ref[t, :, h * 512 + 256:h * 512 + 512] = z[:, 128:].T.astype(BF16)
+            emit(t, h, dot(m2, buf[:, h * 256:(h + 1) * 256]))
 
     first(0, s_a)
 
@@ -205,33 +193,67 @@
             t = UNROLL * i + u
             first(t + 1, s_b)
             second(t, s_a)
-            first(jnp.minimum(t + 2, N_TAU - 1), s_a)
+            first(jnp.minimum(t + 2, count - 1), s_a)
             second(t + 1, s_b)
         return carry
 
-    lax.fori_loop(0, N_TAU // UNROLL, step, 0)
-
-
-def apply_z(slot, cin, own, far):
-    return pl.pallas_call(
-        functools.partial(z_kernel, slot),
+    lax.fori_loop(0, count // UNROLL, step, 0)
+
+
+def own_kernel(cin_ref, own_ref, zo_ref, fb, bb, s_a, s_b):
+    for j in range(2):
+        part = slice(j * N_TAU, (j + 1) * N_TAU)
+        expand(own_ref[:, j, :, 0:128], False, fb.at[part])
+        expand(own_ref[:, j, :, 128:256], True, bb.at[part])
+
+    def emit(t, h, z):
+        zo_ref[t, :, h * 256:(h + 1) * 256] = z
+
+    pipelined(fb, bb, lambda t: cin_ref[t // N_TAU], emit, s_a, s_b)
+
+
+def own_half(cin, greens):
+    return pl.pallas_call(
+        own_kernel,
+        in_specs=[VM] * 2,
+        out_specs=VM,
+        scratch_shapes=[pltpu.VMEM((2 * N_TAU, 64, 256), BF16)] * 2 + [pltpu.VMEM((256, 512), BF16)] * 2,
+        out_shape=jax.ShapeDtypeStruct((2 * N_TAU, 256, 512), F32),
+        compiler_params=pltpu.CompilerParams(vmem_limit_bytes=24 * 2**20),
+        cost_estimate=pl.CostEstimate(flops=8_000_000_000, bytes_accessed=5_000_000, transcendentals=0),
+    )(cin, greens)
+
+
+def far_kernel(slot, cin_ref, far_ref, zo_ref, z_ref, fb, bb, s_a, s_b):
+    expand(far_ref[0, :, :, 0:128], False, fb)
+    expand(far_ref[0, :, :, 128:256], True, bb)
+
+    def emit(t, h, z):
+        z = z + zo_ref[slot * N_TAU + t, :, h * 256:(h + 1) * 256]
+        z_ref[t, :, h * 512:h * 512 + 256] = z[:, :128].T.astype(BF16)
+        z_ref[t, :, h * 512 + 256:h * 512 + 512] = z[:, 128:].T.astype(BF16)
+
+    pipelined(fb, bb, lambda t: cin_ref[slot], emit, s_a, s_b)
+
+
+def far_half(slot, cin, far, zo):
+    return pl.pallas_call(
+        functools.partial(far_kernel, slot),
         in_specs=[VM] * 3,
         out_specs=VM,
-        scratch_shapes=[pltpu.VMEM((N_TAU, 2, 64, 256), BF16)] * 2
-        + [pltpu.VMEM((512, 512), BF16)] * 2,
+        scratch_shapes=[pltpu.VMEM((N_TAU, 64, 256), BF16)] * 2 + [pltpu.VMEM((256, 512), BF16)] * 2,
         out_shape=jax.ShapeDtypeStruct((N_TAU, AUX, 1024), BF16),
-        compiler_params=pltpu.CompilerParams(vmem_limit_bytes=16 * 2**20),
-        cost_estimate=pl.CostEstimate(flops=8_000_000_000, bytes_accessed=5_000_000, transcendentals=0),
-    )(cin, own, far)
-
-
-def last_kernel(c0_ref, c1a_ref, c1b_ref, z0_ref, z1_ref, out_ref, cp):
+        compiler_params=pltpu.CompilerParams(vmem_limit_bytes=24 * 2**20),
+        cost_estimate=pl.CostEstimate(flops=4_000_000_000, bytes_accessed=5_000_000, transcendentals=0),
+    )(cin, far, zo)
+
+
+def last_kernel(c0_ref, c1_ref, z0_ref, z1_ref, out_ref, cp):
     r = lax.broadcasted_iota(jnp.int32, (256, 256), 0)
     q = lax.broadcasted_iota(jnp.int32, (256, 256), 1)
     pm = jnp.where(q == (r % 32 // 8) * 64 + (r % 8) * 8 + r // 32, 1.0, 0.0).astype(BF16)
-    for j in range(2):
-        atom = c0_ref[0] if j == 0 else jnp.concatenate([c1a_ref[0], c1b_ref[0]], axis=0)
-        turned = [dot(atom[:, a * 256:(a + 1) * 256], pm) for a in range(4)]
+    for j, ref in enumerate((c0_ref, c1_ref)):
+        turned = [dot(ref[0, :, a * 256:(a + 1) * 256], pm) for a in range(4)]
         for h in range(4):
             cp[j, :, h * 256:(h + 1) * 256] = jnp.concatenate(
                 [turned[a][:, h * 64:(h + 1) * 64] for a in range(4)], axis=1
@@ -251,16 +273,16 @@
     lax.fori_loop(0, N_TAU // 4, step, 0)
 
 
-def last_product(c0, c1a, c1b, z0, z1):
+def last_product(c0, c1, z0, z1):
     return pl.pallas_call(
         last_kernel,
-        in_specs=[VM] * 5,
+        in_specs=[VM] * 4,
         out_specs=VM,
         scratch_shapes=[pltpu.VMEM((2, AUX, 1024), BF16)],
         out_shape=jax.ShapeDtypeStruct((N_TAU, 2, AUX, AUX), BF16),
         compiler_params=pltpu.CompilerParams(vmem_limit_bytes=16 * 2**20),
         cost_estimate=pl.CostEstimate(flops=1_200_000_000, bytes_accessed=10_000_000, transcendentals=0),
-    )(c0, c1a, c1b, z0, z1)
+    )(c0, c1, z0, z1)
 
 
 def finish_kernel(partner_ref, column_ref, in_ref, out_ref):
@@ -297,17 +319,15 @@
 
 
 def body(coeff, green_fwd, green_bwd, home_atom, send_atoms, partner, mirror):
-    send, atom0, atom1a, atom1b = prepare(partner, send_atoms, coeff, green_fwd[:, 0, :], green_bwd[:, 0, :])
+    send, atoms = prepare(partner, send_atoms, coeff, green_fwd[:, 0, :], green_bwd[:, 0, :])
+    bulk = send_z(atoms)
     greens = exchange(send).reshape(N_TAU, 2, 8, 512)
-    c1a = send_z(atom1a)
     cin = turn_home(partner, home_atom, coeff)
-    outgoing, atom0, atom1b = lax.optimization_barrier((greens[:, :, :, 256:512].transpose(1, 0, 2, 3), atom0, atom1b))
-    far = send_z(outgoing)
-    c1b = send_z(atom1b)
-    c0 = send_z(atom0)
-    z0 = apply_z(0, cin, greens, far)
-    z1 = apply_z(1, cin, greens, swap(far[1:2]))
-    tiles = last_product(c0, swap(c1a), swap(c1b), z0, z1)
+    far = send_z(greens[:, :, :, 256:512].transpose(1, 0, 2, 3))
+    zo = own_half(cin, greens)
+    z0 = far_half(0, cin, far, zo)
+    z1 = far_half(1, cin, swap(far[1:2]), zo)
+    tiles = last_product(bulk, swap(bulk[1:2]), z0, z1)
     back = exchange(tiles.reshape(32, AUX, AUX))
     return finish(partner, back).reshape(32, 1, AUX, AUX)
 

time: 103 us -> 108 us (1.049)
  the two profiles are of different devices: /device:TPU:64 before, /device:TPU:32 now
where the time goes in v4:
time: 108 us; the launch traced here: 107 us
  blocking collectives  44.1 us (41%)
  starting transfers between devices  31.9 us (30%)
  Pallas kernels  24.2 us (22%)
  waiting for transfers between devices  5.67 us (5%)
  local copies, waits for them, and re-layouts  1.08 us (1%)
    all_to_all x1, blocking collectives, exchange(): return lax.all_to_all(x, 'tau', split_axis=0, concat_axis=0, tiled=True)  44.1 us
    ppermute x2, starting transfers between devices, send_z(): return lax.ppermute(x, BOTH, ALONG_Z)  20.5 us
    all_to_all x1, starting transfers between devices, exchange(): return lax.all_to_all(x, 'tau', split_axis=0, concat_axis=0, tiled=True)  7.04 us
    pallas_call x2, Pallas kernels, far_half(): pl.pallas_call(functools.partial(far_kernel, slot), in_specs=[VM] * 3, ou...  6.84 us
    pallas_call x1, Pallas kernels, own_half(): pl.pallas_call(own_kernel, in_specs=[VM] * 2, out_specs=VM, scratch_shape...  6.2 us
    ppermute x2, waiting for transfers between devices, send_z(): return lax.ppermute(x, BOTH, ALONG_Z)  5.66 us
    ppermute x2, starting transfers between devices, swap(): return lax.ppermute(x, 'pair', SWAP)  4.31 us
    pallas_call x1, Pallas kernels, last_product(): pl.pallas_call(last_kernel, in_specs=[VM] * 4, out_specs=VM, scratch_shap...  3.26 us
  transfers between devices with their start and end apart: 5, of which 1 were waited for; matrix products, arithmetic and copies ran while one was open for 0% of the time, Pallas kernels for 14%

profile of v4, /device:TPU:32, one launch (start us, length us, event | category | flops | bytes accessed | tf_op | source)
XLA Modules:
  0.0 107.1 jit_solution(17704231914373549640)
XLA Ops:
  0.0 3.1 %shard_map.109 = (bf16[32,8,512]{2,1,0:T(8,128)(2,1)}, bf16[2,128,1024]{2,1,0:T(8,128)(2,1)}) custom-call(s32[32]{0:T(128)} %asked_ref.1, s32[256]{0:T(256)} %constant.10.clone.dst_ref, f32[32,32]{1,0:T(8,128)} %constant.11.clone.near_ref, f32[32,32]{1,0:T(8,128)} %constant.12.clone.away_ref, s32[1,32]{1,0:T(1,128)} %bitcast.13, ...), custom_call_target="tpu_custom_call" | custom-call | flops 200000000 | bytes 3000000 | tf_op jit(solution)/shard_map/pallas_call | solution.py:108
  3.1 7.0 %all-to-all-start = ((bf16[32,8,512]{2,1,0:T(8,128)(2,1)}), bf16[32,8,512]{2,1,0:T(8,128)(2,1)S(1)}, u32[]{:S(2)}, u32[]{:S(2)}) async-start(bf16[32,8,512]{2,1,0:T(8,128)(2,1)} %get-tuple-element.8), calls=%async_computation | async-start | bytes 524288 | tf_op jit(solution)/shard_map/all_to_all | solution.py:310
  10.2 14.4 %collective-permute-start = (bf16[2,128,1024]{2,1,0:T(8,128)(2,1)}, bf16[2,128,1024]{2,1,0:T(8,128)(2,1)S(1)}, u32[]{:S(2)}, u32[]{:S(2)}) collective-permute-start(bf16[2,128,1024]{2,1,0:T(8,128)(2,1)} %get-tuple-element.7), channel_id=1, source_target_pairs={{0,32},{1,225},{2,290},{3,483},{4,68},{5,453},{6,198},{7,327},{8,1... | collective-permute-start | bytes 1572872 | tf_op jit(solution)/shard_map/ppermute | solution.py:314
  24.5 2.3 %shard_map.110.cin_ref = bf16[2,256,512]{2,1,0:T(8,128)(2,1)} custom-call(s32[32]{0:T(128)} %partner_ref.3, s32[32]{0:T(128)} %homes_ref.1, s32[256]{0:T(256)} %constant.13.clone.src_ref, bf16[4,128,1024]{2,1,0:T(8,128)(2,1)} %coeff_ref.3), custom_call_target="tpu_custom_call" | custom-call | flops 100000000 | bytes 2000000 | tf_op jit(solution)/shard_map/pallas_call | solution.py:143
  26.8 0.0 all-to-all-done
  26.9 6.2 %collective-permute-start.2 = (bf16[2,16,8,256]{3,2,1,0:T(8,128)(2,1)S(1)}, bf16[2,16,8,256]{3,2,1,0:T(8,128)(2,1)S(1)}, u32[]{:S(2)}, u32[]{:S(2)}) collective-permute-start(bf16[2,16,8,256]{3,2,1,0:T(8,128)(2,1)S(1)} %copy_bitcast_fusion), channel_id=1, source_target_pairs={{0,32},{1,225},{2,290},{3,483},{4,68},{5,453},{6,198},{7,327},{8,1... | collective-permute-start | bytes 393224 | tf_op jit(solution)/shard_map/ppermute | solution.py:314
  33.0 0.0 copy-start
  33.1 1.0 copy-done
  34.1 6.2 %shard_map.111.zo_ref = f32[32,256,512]{2,1,0:T(8,128)S(1)} custom-call(bf16[2,256,512]{2,1,0:T(8,128)(2,1)S(1)} %copy-done, bf16[16,2,8,512]{3,2,1,0:T(8,128)(2,1)S(1)} %bitcast.12), custom_call_target="tpu_custom_call" | custom-call | flops 8000000000 | bytes 5000000 | tf_op jit(solution)/shard_map/pallas_call | solution.py:216
  40.3 5.7 %collective-permute-done.2.far_ref = bf16[2,16,8,256]{3,2,1,0:T(8,128)(2,1)S(1)} collective-permute-done((bf16[2,16,8,256]{3,2,1,0:T(8,128)(2,1)S(1)}, bf16[2,16,8,256]{3,2,1,0:T(8,128)(2,1)S(1)}, u32[]{:S(2)}, u32[]{:S(2)}) %collective-permute-start.2) | collective-permute-done | bytes 131104 | tf_op jit(solution)/shard_map/ppermute | solution.py:314
  46.0 1.9 %collective-permute-start.3 = (bf16[1,16,8,256]{3,2,1,0:T(8,128)(2,1)S(1)}, bf16[1,16,8,256]{3,2,1,0:T(8,128)(2,1)S(1)}, u32[]{:S(2)}, u32[]{:S(2)}) collective-permute-start(bf16[1,16,8,256]{3,2,1,0:T(8,128)(2,1)S(1)} %slice.14), channel_id=1, source_target_pairs={{0,16},{16,0},{32,48},{48,32},{64,80},{80,64},{96,112},{112,96},{1... | collective-permute-start | bytes 196616 | tf_op jit(solution)/shard_map/ppermute | solution.py:318
  47.9 3.4 %shard_map.112.z0_ref = bf16[16,128,1024]{2,1,0:T(8,128)(2,1)S(1)} custom-call(bf16[2,256,512]{2,1,0:T(8,128)(2,1)S(1)} %copy-done, bf16[2,16,8,256]{3,2,1,0:T(8,128)(2,1)S(1)} %collective-permute-done.2.far_ref, f32[32,256,512]{2,1,0:T(8,128)S(1)} %shard_map.111.zo_ref), custom_call_target="tpu_custom_call" | custom-call | flops 4000000000 | bytes 5000000 | tf_op jit(solution)/shard_map/pallas_call | solution.py:240
  51.3 0.0 collective-permute-done.c0_ref
  51.3 2.4 %collective-permute-start.1 = (bf16[1,128,1024]{2,1,0:T(8,128)(2,1)S(1)}, bf16[1,128,1024]{2,1,0:T(8,128)(2,1)S(1)}, u32[]{:S(2)}, u32[]{:S(2)}) collective-permute-start(bf16[1,128,1024]{2,1,0:T(8,128)(2,1)S(1)} %slice.12), channel_id=1, source_target_pairs={{0,16},{16,0},{32,48},{48,32},{64,80},{80,64},{96,112},{112,96},{1... | collective-permute-start | bytes 786440 | tf_op jit(solution)/shard_map/ppermute | solution.py:318
  53.8 0.0 collective-permute-done.3.far_ref
  53.8 3.4 %shard_map.113.z1_ref = bf16[16,128,1024]{2,1,0:T(8,128)(2,1)S(1)} custom-call(bf16[2,256,512]{2,1,0:T(8,128)(2,1)S(1)} %copy-done, bf16[1,16,8,256]{3,2,1,0:T(8,128)(2,1)S(1)} %collective-permute-done.3.far_ref, f32[32,256,512]{2,1,0:T(8,128)S(1)} %shard_map.111.zo_ref), custom_call_target="tpu_custom_call" | custom-call | flops 4000000000 | bytes 5000000 | tf_op jit(solution)/shard_map/pallas_call | solution.py:240
  57.2 0.0 copy-start.1
  57.2 0.0 copy-start.2
  57.2 0.0 collective-permute-done.1.c1_ref
  57.2 3.3 %shard_map.114 = bf16[16,2,128,128]{3,2,1,0:T(8,128)(2,1)S(1)} custom-call(bf16[2,128,1024]{2,1,0:T(8,128)(2,1)S(1)} %collective-permute-done.c0_ref, bf16[1,128,1024]{2,1,0:T(8,128)(2,1)S(1)} %collective-permute-done.1.c1_ref, bf16[16,128,1024]{2,1,0:T(8,128)(2,1)S(1)} %shard_map.112.z0_ref, bf16[16,128,1024]{2,1,0:T(8,128)(2,1)S(1)} %shard_map.113.z1_ref), custom_call_target="tpu_custom_call" | custom-call | flops 1200000000 | bytes 10000000 | tf_op jit(solution)/shard_map/pallas_call | solution.py:277
  60.5 44.1 %all_to_all.10.in_ref = bf16[32,128,128]{2,1,0:T(8,128)(2,1)S(1)} all-to-all(bf16[32,128,128]{2,1,0:T(8,128)(2,1)S(1)} %bitcast.10), channel_id=1, replica_groups=mesh['pair'=32,'tau'=16] {'tau'}, dimensions={0} | all-to-all | bytes 2097152 | tf_op jit(solution)/shard_map/all_to_all | solution.py:310
  104.6 0.0 copy-done.1
  104.6 0.0 copy-done.2
  104.6 2.5 %shard_map.115 = f32[32,128,128]{2,1,0:T(8,128)} custom-call(s32[32]{0:T(128)S(1)} %copy-done.1, s32[256]{0:T(256)S(1)} %copy-done.2, bf16[32,128,128]{2,1,0:T(8,128)(2,1)S(1)} %all_to_all.10.in_ref), custom_call_target="tpu_custom_call" | custom-call | flops 1000000 | bytes 3000000 | tf_op jit(solution)/shard_map/pallas_call | solution.py:298
  (3 shorter events, 0.0 us)
Async XLA Ops:
  3.1 23.7 %all-to-all-start = ((bf16[32,8,512]{2,1,0:T(8,128)(2,1)}), bf16[32,8,512]{2,1,0:T(8,128)(2,1)S(1)}, u32[]{:S(2)}, u32[]{:S(2)}) async-start(bf16[32,8,512]{2,1,0:T(8,128)(2,1)} %get-tuple-element.8), calls=%async_computation | async-start | bytes 524288 | tf_op jit(solution)/shard_map/all_to_all | solution.py:310
  10.2 41.2 %collective-permute-start = (bf16[2,128,1024]{2,1,0:T(8,128)(2,1)}, bf16[2,128,1024]{2,1,0:T(8,128)(2,1)S(1)}, u32[]{:S(2)}, u32[]{:S(2)}) collective-permute-start(bf16[2,128,1024]{2,1,0:T(8,128)(2,1)} %get-tuple-element.7), channel_id=1, source_target_pairs={{0,32},{1,225},{2,290},{3,483},{4,68},{5,453},{6,198},{7,327},{8,1... | collective-permute-start | bytes 1572872 | tf_op jit(solution)/shard_map/ppermute | solution.py:314
  26.9 19.1 %collective-permute-start.2 = (bf16[2,16,8,256]{3,2,1,0:T(8,128)(2,1)S(1)}, bf16[2,16,8,256]{3,2,1,0:T(8,128)(2,1)S(1)}, u32[]{:S(2)}, u32[]{:S(2)}) collective-permute-start(bf16[2,16,8,256]{3,2,1,0:T(8,128)(2,1)S(1)} %copy_bitcast_fusion), channel_id=1, source_target_pairs={{0,32},{1,225},{2,290},{3,483},{4,68},{5,453},{6,198},{7,327},{8,1... | collective-permute-start | bytes 393224 | tf_op jit(solution)/shard_map/ppermute | solution.py:314
  33.0 1.0 copy-start
  46.0 7.8 %collective-permute-start.3 = (bf16[1,16,8,256]{3,2,1,0:T(8,128)(2,1)S(1)}, bf16[1,16,8,256]{3,2,1,0:T(8,128)(2,1)S(1)}, u32[]{:S(2)}, u32[]{:S(2)}) collective-permute-start(bf16[1,16,8,256]{3,2,1,0:T(8,128)(2,1)S(1)} %slice.14), channel_id=1, source_target_pairs={{0,16},{16,0},{32,48},{48,32},{64,80},{80,64},{96,112},{112,96},{1... | collective-permute-start | bytes 196616 | tf_op jit(solution)/shard_map/ppermute | solution.py:318
  51.3 5.9 %collective-permute-start.1 = (bf16[1,128,1024]{2,1,0:T(8,128)(2,1)S(1)}, bf16[1,128,1024]{2,1,0:T(8,128)(2,1)S(1)}, u32[]{:S(2)}, u32[]{:S(2)}) collective-permute-start(bf16[1,128,1024]{2,1,0:T(8,128)(2,1)S(1)} %slice.12), channel_id=1, source_target_pairs={{0,16},{16,0},{32,48},{48,32},{64,80},{80,64},{96,112},{112,96},{1... | collective-permute-start | bytes 786440 | tf_op jit(solution)/shard_map/ppermute | solution.py:318
  57.2 47.4 %copy-start.1 = (s32[32]{0:T(128)S(1)}, s32[32]{0:T(128)}, u32[]{:S(2)}) copy-start(s32[32]{0:T(128)} %partner_ref.3) | copy-start | bytes 388
  57.2 47.4 %copy-start.2 = (s32[256]{0:T(256)S(1)}, s32[256]{0:T(256)}, u32[]{:S(2)}) copy-start(s32[256]{0:T(256)} %constant.14.clone.column_ref) | copy-start | bytes 3076

commit v5 on v4

--- a/solution.py
+++ b/solution.py
@@ -28,26 +28,29 @@
 
 
 def routes():
-    dst = np.zeros((CHIPS, N_TAU), np.int32)
-    src = np.zeros((CHIPS, N_TAU), np.int32)
-    column = np.zeros((CHIPS, CHIPS), np.int32)
-    for z in range(CHIPS):
-        for k in range(N_TAU):
-            to = (z + STEPS[k][z % 4]) % CHIPS
-            dst[z, k] = to
-            src[to, k] = z
-            column[to, z] = k
-    along_z = [
-        ((2 * z + core) * N_TAU + k, (2 * int(dst[z, k]) + core) * N_TAU + k)
-        for z in range(CHIPS)
-        for core in range(2)
-        for k in range(N_TAU)
-    ]
-    return dst, src, column, along_z
-
-
-DST, SRC, COLUMN, ALONG_Z = routes()
-SWAP = [(i, i ^ 1) for i in range(N_PAIR)]
+    dst = np.zeros((2, CHIPS, N_TAU), np.int32)
+    src = np.zeros((2, CHIPS, N_TAU), np.int32)
+    column = np.zeros((2, CHIPS, CHIPS), np.int32)
+    perms = []
+    for j in range(2):
+        for z in range(CHIPS):
+            for k in range(N_TAU):
+                to = (z + STEPS[(k + 8 * j) % N_TAU][z % 4]) % CHIPS
+                dst[j, z, k] = to
+                src[j, to, k] = z
+                column[j, to, z] = k
+        perms.append(
+            [
+                ((2 * z + core) * N_TAU + k, (2 * int(dst[j, z, k]) + (core ^ j)) * N_TAU + k)
+                for z in range(CHIPS)
+                for core in range(2)
+                for k in range(N_TAU)
+            ]
+        )
+    return dst, src, column, perms
+
+
+DST, SRC, COLUMN, PERMS = routes()
 
 
 def dot(a, b):
@@ -59,14 +62,13 @@
 
 
 def prepare_kernel(
-    asked_ref, dst_ref, near_ref, away_ref, peers_ref, coeff_ref, gf_ref, gb_ref, send_ref, atoms_ref,
-    wide
+    asked_ref, dst_ref, near_ref, away_ref, peers_ref, coeff_ref, gf_ref, gb_ref, send_ref, atom0_ref,
+    atom1_ref, wide
 ):
     p, k = lax.axis_index("pair"), lax.axis_index("tau")
-    z, core = p // 2, p % 2
-    to = 2 * dst_ref[z * N_TAU + k]
-    atoms_ref[0] = coeff_ref[asked_ref[to + core]]
-    atoms_ref[1] = coeff_ref[asked_ref[to + 1 - core]]
+    for j, atom_ref in enumerate((atom0_ref, atom1_ref)):
+        to = 2 * dst_ref[(j * CHIPS + p // 2) * N_TAU + k] + (p + j) % 2
+        atom_ref[0] = coeff_ref[asked_ref[to]]
     eye = lax.broadcasted_iota(jnp.int32, (32, 32), 0) == lax.broadcasted_iota(jnp.int32, (32, 32), 1)
     peers = peers_ref[...].astype(F32)
 
@@ -103,16 +105,17 @@
     away = np.zeros((N_PAIR, N_PAIR), np.float32)
     for p in range(N_PAIR):
         for j in range(2):
-            near[p, j::2] = 2 * SRC[p // 2] + (sides[p] ^ j)
-            away[p, j::2] = 2 * DST[p // 2] + (sides[p] ^ j)
+            near[p, j::2] = 2 * SRC[j, p // 2] + (sides[p] ^ j)
+            away[p, j::2] = 2 * DST[j, p // 2] + (sides[p] ^ j)
     return pl.pallas_call(
         prepare_kernel,
         in_specs=[SM] * 2 + [VM] * 6,
-        out_specs=[VM] * 2,
+        out_specs=[VM] * 3,
         scratch_shapes=[pltpu.VMEM((32, 8, 512), F32)],
         out_shape=[
             jax.ShapeDtypeStruct((32, 8, 512), BF16),
-            jax.ShapeDtypeStruct((2, AUX, 1024), BF16),
+            jax.ShapeDtypeStruct((1, AUX, 1024), BF16),
+            jax.ShapeDtypeStruct((1, AUX, 1024), BF16),
         ],
         cost_estimate=pl.CostEstimate(flops=200_000_000, bytes_accessed=3_000_000, transcendentals=0),
     )(
@@ -129,8 +132,8 @@
 
 def turn_kernel(partner_ref, homes_ref, src_ref, coeff_ref, cin_ref):
     p, k = lax.axis_index("pair"), lax.axis_index("tau")
-    come = 2 * src_ref[(p // 2) * N_TAU + k]
     for j in range(2):
+        come = 2 * src_ref[(j * CHIPS + p // 2) * N_TAU + k]
         side = (p + j) % 2
         home = jnp.int32(0)
         for m in range(N_PAIR):
@@ -225,8 +228,8 @@
 
 
 def far_kernel(slot, cin_ref, far_ref, zo_ref, z_ref, fb, bb, s_a, s_b):
-    expand(far_ref[0, :, :, 0:128], False, fb)
-    expand(far_ref[0, :, :, 128:256], True, bb)
+    expand(far_ref[:, :, 0:128], False, fb)
+    expand(far_ref[:, :, 128:256], True, bb)
 
     def emit(t, h, z):
         z = z + zo_ref[slot * N_TAU + t, :, h * 256:(h + 1) * 256]
@@ -290,7 +293,8 @@
     p = lax.axis_index("pair")
     for i in range(8):
         other = partner_ref[base + i]
-        place = 2 * column_ref[(p // 2) * CHIPS + other // 2] + (p + other) % 2
+        j = (p + other) % 2
+        place = 2 * column_ref[(j * CHIPS + p // 2) * CHIPS + other // 2] + j
         out_ref[i] = in_ref[place].astype(F32)
 
 
@@ -310,24 +314,22 @@
     return lax.all_to_all(x, "tau", split_axis=0, concat_axis=0, tiled=True)
 
 
-def send_z(x):
-    return lax.ppermute(x, BOTH, ALONG_Z)
-
-
-def swap(x):
-    return lax.ppermute(x, "pair", SWAP)
+def send_z(x, j):
+    return lax.ppermute(x, BOTH, PERMS[j])
 
 
 def body(coeff, green_fwd, green_bwd, home_atom, send_atoms, partner, mirror):
-    send, atoms = prepare(partner, send_atoms, coeff, green_fwd[:, 0, :], green_bwd[:, 0, :])
-    bulk = send_z(atoms)
+    send, atom0, atom1 = prepare(partner, send_atoms, coeff, green_fwd[:, 0, :], green_bwd[:, 0, :])
+    c0 = send_z(atom0, 0)
+    c1 = send_z(atom1, 1)
     greens = exchange(send).reshape(N_TAU, 2, 8, 512)
     cin = turn_home(partner, home_atom, coeff)
-    far = send_z(greens[:, :, :, 256:512].transpose(1, 0, 2, 3))
+    far0 = send_z(greens[:, 0, :, 256:512], 0)
+    far1 = send_z(greens[:, 1, :, 256:512], 1)
     zo = own_half(cin, greens)
-    z0 = far_half(0, cin, far, zo)
-    z1 = far_half(1, cin, swap(far[1:2]), zo)
-    tiles = last_product(bulk, swap(bulk[1:2]), z0, z1)
+    z0 = far_half(0, cin, far0, zo)
+    z1 = far_half(1, cin, far1, zo)
+    tiles = last_product(c0, c1, z0, z1)
     back = exchange(tiles.reshape(32, AUX, AUX))
     return finish(partner, back).reshape(32, 1, AUX, AUX)
 

time: 108 us -> 93.7 us (0.87)
  the two profiles are of different devices: /device:TPU:32 before, /device:TPU:96 now
where the time goes in v5:
time: 93.7 us; the launch traced here: 93.3 us
  blocking collectives  30.5 us (33%)
  starting transfers between devices  27.1 us (29%)
  Pallas kernels  24.2 us (26%)
  waiting for transfers between devices  10.3 us (11%)
  local copies, waits for them, and re-layouts  1.06 us (1%)
    all_to_all x1, blocking collectives, exchange(): return lax.all_to_all(x, 'tau', split_axis=0, concat_axis=0, tiled=True)  30.5 us
    ppermute x4, starting transfers between devices, send_z(): return lax.ppermute(x, BOTH, PERMS[j])  20.1 us
    ppermute x4, waiting for transfers between devices, send_z(): return lax.ppermute(x, BOTH, PERMS[j])  10.3 us
    all_to_all x1, starting transfers between devices, exchange(): return lax.all_to_all(x, 'tau', split_axis=0, concat_axis=0, tiled=True)  7.04 us
    pallas_call x2, Pallas kernels, far_half(): pl.pallas_call(functools.partial(far_kernel, slot), in_specs=[VM] * 3, ou...  6.84 us
    pallas_call x1, Pallas kernels, own_half(): pl.pallas_call(own_kernel, in_specs=[VM] * 2, out_specs=VM, scratch_shape...  6.18 us
    pallas_call x1, Pallas kernels, last_product(): pl.pallas_call(last_kernel, in_specs=[VM] * 4, out_specs=VM, scratch_shap...  3.26 us
    pallas_call x1, Pallas kernels, prepare(): pl.pallas_call(prepare_kernel, in_specs=[SM] * 2 + [VM] * 6, out_specs=[V...  3.06 us
  transfers between devices with their start and end apart: 5, of which 1 were waited for; matrix products, arithmetic and copies ran while one was open for 0% of the time, Pallas kernels for 16%

profile of v5, /device:TPU:96, one launch (start us, length us, event | category | flops | bytes accessed | tf_op | source)
XLA Modules:
  0.0 93.3 jit_solution(2658306552264597518)
XLA Ops:
  0.0 3.1 %shard_map.109 = (bf16[32,8,512]{2,1,0:T(8,128)(2,1)}, bf16[1,128,1024]{2,1,0:T(8,128)(2,1)}, bf16[1,128,1024]{2,1,0:T(8,128)(2,1)}) custom-call(s32[32]{0:T(128)} %asked_ref.1, s32[512]{0:T(512)} %constant.10.clone.dst_ref, f32[32,32]{1,0:T(8,128)} %constant.11.clone.near_ref, f32[32,32]{1,0:T(8,128)} %constant.12.clone.away_ref, s32[1,32]{1,0:T(1,128)} %bitcast.19, ...), custom_call_target="tpu_custom_call" | custom-call | flops 200000000 | bytes 3000000 | tf_op jit(solution)/shard_map/pallas_call | solution.py:110
  3.1 7.0 %all-to-all-start = ((bf16[32,8,512]{2,1,0:T(8,128)(2,1)}), bf16[32,8,512]{2,1,0:T(8,128)(2,1)S(1)}, u32[]{:S(2)}, u32[]{:S(2)}) async-start(bf16[32,8,512]{2,1,0:T(8,128)(2,1)} %get-tuple-element.10), calls=%async_computation | async-start | bytes 524288 | tf_op jit(solution)/shard_map/all_to_all | solution.py:314
  10.1 2.0 %collective-permute-start = (bf16[1,128,1024]{2,1,0:T(8,128)(2,1)}, bf16[1,128,1024]{2,1,0:T(8,128)(2,1)S(1)}, u32[]{:S(2)}, u32[]{:S(2)}) collective-permute-start(bf16[1,128,1024]{2,1,0:T(8,128)(2,1)} %get-tuple-element.8), channel_id=1, source_target_pairs={{0,32},{1,225},{2,290},{3,483},{4,68},{5,453},{6,198},{7,327},{8,1... | collective-permute-start | bytes 786440 | tf_op jit(solution)/shard_map/ppermute | solution.py:318
  12.1 11.5 %collective-permute-start.1 = (bf16[1,128,1024]{2,1,0:T(8,128)(2,1)}, bf16[1,128,1024]{2,1,0:T(8,128)(2,1)S(1)}, u32[]{:S(2)}, u32[]{:S(2)}) collective-permute-start(bf16[1,128,1024]{2,1,0:T(8,128)(2,1)} %get-tuple-element.9), channel_id=1, source_target_pairs={{0,112},{1,433},{2,178},{3,371},{4,20},{5,149},{6,278},{7,407},{8,... | collective-permute-start | bytes 786440 | tf_op jit(solution)/shard_map/ppermute | solution.py:318
  23.6 2.3 %shard_map.110.cin_ref = bf16[2,256,512]{2,1,0:T(8,128)(2,1)} custom-call(s32[32]{0:T(128)} %partner_ref.3, s32[32]{0:T(128)} %homes_ref.1, s32[512]{0:T(512)} %constant.13.clone.src_ref, bf16[4,128,1024]{2,1,0:T(8,128)(2,1)} %coeff_ref.3), custom_call_target="tpu_custom_call" | custom-call | flops 100000000 | bytes 2000000 | tf_op jit(solution)/shard_map/pallas_call | solution.py:146
  25.9 0.0 all-to-all-done
  25.9 4.7 %collective-permute-start.3 = (bf16[16,8,256]{2,1,0:T(8,128)(2,1)S(1)}, bf16[16,8,256]{2,1,0:T(8,128)(2,1)S(1)}, u32[]{:S(2)}, u32[]{:S(2)}) collective-permute-start(bf16[16,8,256]{2,1,0:T(8,128)(2,1)S(1)} %get-tuple-element.11), channel_id=1, source_target_pairs={{0,112},{1,433},{2,178},{3,371},{4,20},{5,149},{6,278},{7,407},{8,... | collective-permute-start | bytes 196616 | tf_op jit(solution)/shard_map/ppermute | solution.py:318
  30.6 1.9 %collective-permute-start.2 = (bf16[16,8,256]{2,1,0:T(8,128)(2,1)S(1)}, bf16[16,8,256]{2,1,0:T(8,128)(2,1)S(1)}, u32[]{:S(2)}, u32[]{:S(2)}) collective-permute-start(bf16[16,8,256]{2,1,0:T(8,128)(2,1)S(1)} %get-tuple-element.12), channel_id=1, source_target_pairs={{0,32},{1,225},{2,290},{3,483},{4,68},{5,453},{6,198},{7,327},{8,1... | collective-permute-start | bytes 196616 | tf_op jit(solution)/shard_map/ppermute | solution.py:318
  32.5 0.0 copy-start
  32.5 1.0 %copy-done = bf16[2,256,512]{2,1,0:T(8,128)(2,1)S(1)} copy-done((bf16[2,256,512]{2,1,0:T(8,128)(2,1)S(1)}, bf16[2,256,512]{2,1,0:T(8,128)(2,1)}, u32[]{:S(2)}) %copy-start) | copy-done | bytes 524312
  33.6 6.2 %shard_map.111.zo_ref = f32[32,256,512]{2,1,0:T(8,128)S(1)} custom-call(bf16[2,256,512]{2,1,0:T(8,128)(2,1)S(1)} %copy-done, bf16[16,2,8,512]{3,2,1,0:T(8,128)(2,1)S(1)} %bitcast.18), custom_call_target="tpu_custom_call" | custom-call | flops 8000000000 | bytes 5000000 | tf_op jit(solution)/shard_map/pallas_call | solution.py:219
  39.8 10.3 %collective-permute-done.3.far_ref = bf16[16,8,256]{2,1,0:T(8,128)(2,1)S(1)} collective-permute-done((bf16[16,8,256]{2,1,0:T(8,128)(2,1)S(1)}, bf16[16,8,256]{2,1,0:T(8,128)(2,1)S(1)}, u32[]{:S(2)}, u32[]{:S(2)}) %collective-permute-start.3) | collective-permute-done | bytes 65568 | tf_op jit(solution)/shard_map/ppermute | solution.py:318
  50.0 3.4 %shard_map.113.z1_ref = bf16[16,128,1024]{2,1,0:T(8,128)(2,1)S(1)} custom-call(bf16[2,256,512]{2,1,0:T(8,128)(2,1)S(1)} %copy-done, bf16[16,8,256]{2,1,0:T(8,128)(2,1)S(1)} %collective-permute-done.3.far_ref, f32[32,256,512]{2,1,0:T(8,128)S(1)} %shard_map.111.zo_ref), custom_call_target="tpu_custom_call" | custom-call | flops 4000000000 | bytes 5000000 | tf_op jit(solution)/shard_map/pallas_call | solution.py:243
  53.4 0.0 collective-permute-done.2.far_ref
  53.5 3.4 %shard_map.112.z0_ref = bf16[16,128,1024]{2,1,0:T(8,128)(2,1)S(1)} custom-call(bf16[2,256,512]{2,1,0:T(8,128)(2,1)S(1)} %copy-done, bf16[16,8,256]{2,1,0:T(8,128)(2,1)S(1)} %collective-permute-done.2.far_ref, f32[32,256,512]{2,1,0:T(8,128)S(1)} %shard_map.111.zo_ref), custom_call_target="tpu_custom_call" | custom-call | flops 4000000000 | bytes 5000000 | tf_op jit(solution)/shard_map/pallas_call | solution.py:243
  56.9 0.0 copy-start.1
  56.9 0.0 copy-start.2
  56.9 0.0 collective-permute-done.c0_ref
  56.9 0.0 collective-permute-done.1.c1_ref
  56.9 3.3 %shard_map.114 = bf16[16,2,128,128]{3,2,1,0:T(8,128)(2,1)S(1)} custom-call(bf16[1,128,1024]{2,1,0:T(8,128)(2,1)S(1)} %collective-permute-done.c0_ref, bf16[1,128,1024]{2,1,0:T(8,128)(2,1)S(1)} %collective-permute-done.1.c1_ref, bf16[16,128,1024]{2,1,0:T(8,128)(2,1)S(1)} %shard_map.112.z0_ref, bf16[16,128,1024]{2,1,0:T(8,128)(2,1)S(1)} %shard_map.113.z1_ref), custom_call_target="tpu_custom_call" | custom-call | flops 1200000000 | bytes 10000000 | tf_op jit(solution)/shard_map/pallas_call | solution.py:280
  60.2 30.5 %all_to_all.10.in_ref = bf16[32,128,128]{2,1,0:T(8,128)(2,1)S(1)} all-to-all(bf16[32,128,128]{2,1,0:T(8,128)(2,1)S(1)} %bitcast.16), channel_id=1, replica_groups=mesh['pair'=32,'tau'=16] {'tau'}, dimensions={0} | all-to-all | bytes 2097152 | tf_op jit(solution)/shard_map/all_to_all | solution.py:314
  90.7 0.0 copy-done.1
  90.7 0.0 copy-done.2
  90.7 2.6 %shard_map.115 = f32[32,128,128]{2,1,0:T(8,128)} custom-call(s32[32]{0:T(128)S(1)} %copy-done.1, s32[512]{0:T(512)S(1)} %copy-done.2, bf16[32,128,128]{2,1,0:T(8,128)(2,1)S(1)} %all_to_all.10.in_ref), custom_call_target="tpu_custom_call" | custom-call | flops 1000000 | bytes 3000000 | tf_op jit(solution)/shard_map/pallas_call | solution.py:302
  (1 shorter events, 0.0 us)
Async XLA Ops:
  3.1 22.8 %all-to-all-start = ((bf16[32,8,512]{2,1,0:T(8,128)(2,1)}), bf16[32,8,512]{2,1,0:T(8,128)(2,1)S(1)}, u32[]{:S(2)}, u32[]{:S(2)}) async-start(bf16[32,8,512]{2,1,0:T(8,128)(2,1)} %get-tuple-element.10), calls=%async_computation | async-start | bytes 524288 | tf_op jit(solution)/shard_map/all_to_all | solution.py:314
  10.1 46.8 %collective-permute-start = (bf16[1,128,1024]{2,1,0:T(8,128)(2,1)}, bf16[1,128,1024]{2,1,0:T(8,128)(2,1)S(1)}, u32[]{:S(2)}, u32[]{:S(2)}) collective-permute-start(bf16[1,128,1024]{2,1,0:T(8,128)(2,1)} %get-tuple-element.8), channel_id=1, source_target_pairs={{0,32},{1,225},{2,290},{3,483},{4,68},{5,453},{6,198},{7,327},{8,1... | collective-permute-start | bytes 786440 | tf_op jit(solution)/shard_map/ppermute | solution.py:318
  12.1 44.8 %collective-permute-start.1 = (bf16[1,128,1024]{2,1,0:T(8,128)(2,1)}, bf16[1,128,1024]{2,1,0:T(8,128)(2,1)S(1)}, u32[]{:S(2)}, u32[]{:S(2)}) collective-permute-start(bf16[1,128,1024]{2,1,0:T(8,128)(2,1)} %get-tuple-element.9), channel_id=1, source_target_pairs={{0,112},{1,433},{2,178},{3,371},{4,20},{5,149},{6,278},{7,407},{8,... | collective-permute-start | bytes 786440 | tf_op jit(solution)/shard_map/ppermute | solution.py:318
  25.9 24.1 %collective-permute-start.3 = (bf16[16,8,256]{2,1,0:T(8,128)(2,1)S(1)}, bf16[16,8,256]{2,1,0:T(8,128)(2,1)S(1)}, u32[]{:S(2)}, u32[]{:S(2)}) collective-permute-start(bf16[16,8,256]{2,1,0:T(8,128)(2,1)S(1)} %get-tuple-element.11), channel_id=1, source_target_pairs={{0,112},{1,433},{2,178},{3,371},{4,20},{5,149},{6,278},{7,407},{8,... | collective-permute-start | bytes 196616 | tf_op jit(solution)/shard_map/ppermute | solution.py:318
  30.6 22.9 %collective-permute-start.2 = (bf16[16,8,256]{2,1,0:T(8,128)(2,1)S(1)}, bf16[16,8,256]{2,1,0:T(8,128)(2,1)S(1)}, u32[]{:S(2)}, u32[]{:S(2)}) collective-permute-start(bf16[16,8,256]{2,1,0:T(8,128)(2,1)S(1)} %get-tuple-element.12), channel_id=1, source_target_pairs={{0,32},{1,225},{2,290},{3,483},{4,68},{5,453},{6,198},{7,327},{8,1... | collective-permute-start | bytes 196616 | tf_op jit(solution)/shard_map/ppermute | solution.py:318
  32.5 1.0 %copy-start = (bf16[2,256,512]{2,1,0:T(8,128)(2,1)S(1)}, bf16[2,256,512]{2,1,0:T(8,128)(2,1)}, u32[]{:S(2)}) copy-start(bf16[2,256,512]{2,1,0:T(8,128)(2,1)} %shard_map.110.cin_ref) | copy-start | bytes 1572868
  56.9 33.8 %copy-start.1 = (s32[32]{0:T(128)S(1)}, s32[32]{0:T(128)}, u32[]{:S(2)}) copy-start(s32[32]{0:T(128)} %partner_ref.3) | copy-start | bytes 388
  56.9 33.8 %copy-start.2 = (s32[512]{0:T(512)S(1)}, s32[512]{0:T(512)}, u32[]{:S(2)}) copy-start(s32[512]{0:T(512)} %constant.14.clone.column_ref) | copy-start | bytes 6148

commit v6 on v5

--- a/solution.py
+++ b/solution.py
@@ -63,12 +63,14 @@
 
 def prepare_kernel(
     asked_ref, dst_ref, near_ref, away_ref, peers_ref, coeff_ref, gf_ref, gb_ref, send_ref, atom0_ref,
-    atom1_ref, wide
+    atom1a_ref, atom1b_ref, wide
 ):
     p, k = lax.axis_index("pair"), lax.axis_index("tau")
-    for j, atom_ref in enumerate((atom0_ref, atom1_ref)):
-        to = 2 * dst_ref[(j * CHIPS + p // 2) * N_TAU + k] + (p + j) % 2
-        atom_ref[0] = coeff_ref[asked_ref[to]]
+    to = [2 * dst_ref[(j * CHIPS + p // 2) * N_TAU + k] + (p + j) % 2 for j in range(2)]
+    atom0_ref[0] = coeff_ref[asked_ref[to[0]]]
+    other = asked_ref[to[1]]
+    atom1a_ref[0] = coeff_ref[other, :64]
+    atom1b_ref[0] = coeff_ref[other, 64:]
     eye = lax.broadcasted_iota(jnp.int32, (32, 32), 0) == lax.broadcasted_iota(jnp.int32, (32, 32), 1)
     peers = peers_ref[...].astype(F32)
 
@@ -110,12 +112,13 @@
     return pl.pallas_call(
         prepare_kernel,
         in_specs=[SM] * 2 + [VM] * 6,
-        out_specs=[VM] * 3,
+        out_specs=[VM] * 4,
         scratch_shapes=[pltpu.VMEM((32, 8, 512), F32)],
         out_shape=[
             jax.ShapeDtypeStruct((32, 8, 512), BF16),
             jax.ShapeDtypeStruct((1, AUX, 1024), BF16),
-            jax.ShapeDtypeStruct((1, AUX, 1024), BF16),
+            jax.ShapeDtypeStruct((1, 64, 1024), BF16),
+            jax.ShapeDtypeStruct((1, 64, 1024), BF16),
         ],
         cost_estimate=pl.CostEstimate(flops=200_000_000, bytes_accessed=3_000_000, transcendentals=0),
     )(
@@ -251,12 +254,13 @@
     )(cin, far, zo)
 
 
-def last_kernel(c0_ref, c1_ref, z0_ref, z1_ref, out_ref, cp):
+def last_kernel(c0_ref, c1a_ref, c1b_ref, z0_ref, z1_ref, out_ref, cp):
     r = lax.broadcasted_iota(jnp.int32, (256, 256), 0)
     q = lax.broadcasted_iota(jnp.int32, (256, 256), 1)
     pm = jnp.where(q == (r % 32 // 8) * 64 + (r % 8) * 8 + r // 32, 1.0, 0.0).astype(BF16)
-    for j, ref in enumerate((c0_ref, c1_ref)):
-        turned = [dot(ref[0, :, a * 256:(a + 1) * 256], pm) for a in range(4)]
+    for j in range(2):
+        atom = c0_ref[0] if j == 0 else jnp.concatenate([c1a_ref[0], c1b_ref[0]], axis=0)
+        turned = [dot(atom[:, a * 256:(a + 1) * 256], pm) for a in range(4)]
         for h in range(4):
             cp[j, :, h * 256:(h + 1) * 256] = jnp.concatenate(
                 [turned[a][:, h * 64:(h + 1) * 64] for a in range(4)], axis=1
@@ -276,16 +280,16 @@
     lax.fori_loop(0, N_TAU // 4, step, 0)
 
 
-def last_product(c0, c1, z0, z1):
+def last_product(c0, c1a, c1b, z0, z1):
     return pl.pallas_call(
         last_kernel,
-        in_specs=[VM] * 4,
+        in_specs=[VM] * 5,
         out_specs=VM,
         scratch_shapes=[pltpu.VMEM((2, AUX, 1024), BF16)],
         out_shape=jax.ShapeDtypeStruct((N_TAU, 2, AUX, AUX), BF16),
         compiler_params=pltpu.CompilerParams(vmem_limit_bytes=16 * 2**20),
         cost_estimate=pl.CostEstimate(flops=1_200_000_000, bytes_accessed=10_000_000, transcendentals=0),
-    )(c0, c1, z0, z1)
+    )(c0, c1a, c1b, z0, z1)
 
 
 def finish_kernel(partner_ref, column_ref, in_ref, out_ref):
@@ -319,9 +323,10 @@
 
 
 def body(coeff, green_fwd, green_bwd, home_atom, send_atoms, partner, mirror):
-    send, atom0, atom1 = prepare(partner, send_atoms, coeff, green_fwd[:, 0, :], green_bwd[:, 0, :])
+    send, atom0, atom1a, atom1b = prepare(partner, send_atoms, coeff, green_fwd[:, 0, :], green_bwd[:, 0, :])
     c0 = send_z(atom0, 0)
-    c1 = send_z(atom1, 1)
+    c1a = send_z(atom1a, 1)
+    c1b = send_z(atom1b, 1)
     greens = exchange(send).reshape(N_TAU, 2, 8, 512)
     cin = turn_home(partner, home_atom, coeff)
     far0 = send_z(greens[:, 0, :, 256:512], 0)
@@ -329,7 +334,7 @@
     zo = own_half(cin, greens)
     z0 = far_half(0, cin, far0, zo)
     z1 = far_half(1, cin, far1, zo)
-    tiles = last_product(c0, c1, z0, z1)
+    tiles = last_product(c0, c1a, c1b, z0, z1)
     back = exchange(tiles.reshape(32, AUX, AUX))
     return finish(partner, back).reshape(32, 1, AUX, AUX)
 

time: 93.7 us -> 102 us (1.089)
  the two profiles are of different devices: /device:TPU:96 before, /device:TPU:1 now
where the time goes in v6:
time: 102 us; the launch traced here: 101 us
  starting transfers between devices  39.4 us (39%)
  blocking collectives  32.2 us (32%)
  Pallas kernels  24.3 us (24%)
  waiting for transfers between devices  4.09 us (4%)
  local copies, waits for them, and re-layouts  1.06 us (1%)
    all_to_all x1, blocking collectives, exchange(): return lax.all_to_all(x, 'tau', split_axis=0, concat_axis=0, tiled=True)  32.2 us
    ppermute x5, starting transfers between devices, send_z(): return lax.ppermute(x, BOTH, PERMS[j])  31.8 us
    all_to_all x1, starting transfers between devices, exchange(): return lax.all_to_all(x, 'tau', split_axis=0, concat_axis=0, tiled=True)  7.57 us
    pallas_call x2, Pallas kernels, far_half(): pl.pallas_call(functools.partial(far_kernel, slot), in_specs=[VM] * 3, ou...  6.84 us
    pallas_call x1, Pallas kernels, own_half(): pl.pallas_call(own_kernel, in_specs=[VM] * 2, out_specs=VM, scratch_shape...  6.19 us
    ppermute x5, waiting for transfers between devices, send_z(): return lax.ppermute(x, BOTH, PERMS[j])  4.09 us
    pallas_call x1, Pallas kernels, last_product(): pl.pallas_call(last_kernel, in_specs=[VM] * 5, out_specs=VM, scratch_shap...  3.28 us
    pallas_call x1, Pallas kernels, prepare(): pl.pallas_call(prepare_kernel, in_specs=[SM] * 2 + [VM] * 6, out_specs=[V...  3.06 us
  transfers between devices with their start and end apart: 6, of which 2 were waited for; matrix products, arithmetic and copies ran while one was open for 0% of the time, Pallas kernels for 15%

profile of v6, /device:TPU:1, one launch (start us, length us, event | category | flops | bytes accessed | tf_op | source)
XLA Modules:
  0.0 101.1 jit_solution(3145734883223980007)
XLA Ops:
  0.0 3.1 %shard_map.109 = (bf16[32,8,512]{2,1,0:T(8,128)(2,1)}, bf16[1,128,1024]{2,1,0:T(8,128)(2,1)}, bf16[1,64,1024]{2,1,0:T(8,128)(2,1)}, bf16[1,64,1024]{2,1,0:T(8,128)(2,1)}) custom-call(s32[32]{0:T(128)} %asked_ref.1, s32[512]{0:T(512)} %constant.10.clone.dst_ref, f32[32,32]{1,0:T(8,128)} %constant.11.clone.near_ref, f32[32,32]{1,0:T(8,128)} %constant.12.clone.away_ref, ...), custom_call_target="tpu_custom_call" | custom-call | flops 200000000 | bytes 3000000 | tf_op jit(solution)/shard_map/pallas_call | solution.py:112
  3.1 7.6 %all-to-all-start = ((bf16[32,8,512]{2,1,0:T(8,128)(2,1)}), bf16[32,8,512]{2,1,0:T(8,128)(2,1)S(1)}, u32[]{:S(2)}, u32[]{:S(2)}) async-start(bf16[32,8,512]{2,1,0:T(8,128)(2,1)} %get-tuple-element.12), calls=%async_computation | async-start | bytes 524288 | tf_op jit(solution)/shard_map/all_to_all | solution.py:318
  10.6 7.1 %collective-permute-start.1 = (bf16[1,64,1024]{2,1,0:T(8,128)(2,1)}, bf16[1,64,1024]{2,1,0:T(8,128)(2,1)S(1)}, u32[]{:S(2)}, u32[]{:S(2)}) collective-permute-start(bf16[1,64,1024]{2,1,0:T(8,128)(2,1)} %get-tuple-element.10), channel_id=1, source_target_pairs={{0,112},{1,433},{2,178},{3,371},{4,20},{5,149},{6,278},{7,407},{8,... | collective-permute-start | bytes 393224 | tf_op jit(solution)/shard_map/ppermute | solution.py:322
  17.7 10.8 %collective-permute-start.2 = (bf16[1,64,1024]{2,1,0:T(8,128)(2,1)}, bf16[1,64,1024]{2,1,0:T(8,128)(2,1)S(1)}, u32[]{:S(2)}, u32[]{:S(2)}) collective-permute-start(bf16[1,64,1024]{2,1,0:T(8,128)(2,1)} %get-tuple-element.11), channel_id=1, source_target_pairs={{0,112},{1,433},{2,178},{3,371},{4,20},{5,149},{6,278},{7,407},{8,... | collective-permute-start | bytes 393224 | tf_op jit(solution)/shard_map/ppermute | solution.py:322
  28.6 2.6 %collective-permute-start = (bf16[1,128,1024]{2,1,0:T(8,128)(2,1)}, bf16[1,128,1024]{2,1,0:T(8,128)(2,1)S(1)}, u32[]{:S(2)}, u32[]{:S(2)}) collective-permute-start(bf16[1,128,1024]{2,1,0:T(8,128)(2,1)} %get-tuple-element.9), channel_id=1, source_target_pairs={{0,32},{1,225},{2,290},{3,483},{4,68},{5,453},{6,198},{7,327},{8,1... | collective-permute-start | bytes 786440 | tf_op jit(solution)/shard_map/ppermute | solution.py:322
  31.2 2.3 %shard_map.110.cin_ref = bf16[2,256,512]{2,1,0:T(8,128)(2,1)} custom-call(s32[32]{0:T(128)} %partner_ref.3, s32[32]{0:T(128)} %homes_ref.1, s32[512]{0:T(512)} %constant.13.clone.src_ref, bf16[4,128,1024]{2,1,0:T(8,128)(2,1)} %coeff_ref.3), custom_call_target="tpu_custom_call" | custom-call | flops 100000000 | bytes 2000000 | tf_op jit(solution)/shard_map/pallas_call | solution.py:149
  33.5 0.0 all-to-all-done
  33.6 4.7 %collective-permute-start.4 = (bf16[16,8,256]{2,1,0:T(8,128)(2,1)S(1)}, bf16[16,8,256]{2,1,0:T(8,128)(2,1)S(1)}, u32[]{:S(2)}, u32[]{:S(2)}) collective-permute-start(bf16[16,8,256]{2,1,0:T(8,128)(2,1)S(1)} %get-tuple-element.13), channel_id=1, source_target_pairs={{0,112},{1,433},{2,178},{3,371},{4,20},{5,149},{6,278},{7,407},{8,... | collective-permute-start | bytes 196616 | tf_op jit(solution)/shard_map/ppermute | solution.py:322
  38.2 6.6 %collective-permute-start.3 = (bf16[16,8,256]{2,1,0:T(8,128)(2,1)S(1)}, bf16[16,8,256]{2,1,0:T(8,128)(2,1)S(1)}, u32[]{:S(2)}, u32[]{:S(2)}) collective-permute-start(bf16[16,8,256]{2,1,0:T(8,128)(2,1)S(1)} %get-tuple-element.14), channel_id=1, source_target_pairs={{0,32},{1,225},{2,290},{3,483},{4,68},{5,453},{6,198},{7,327},{8,1... | collective-permute-start | bytes 196616 | tf_op jit(solution)/shard_map/ppermute | solution.py:322
  44.8 0.0 copy-start
  44.8 1.0 %copy-done = bf16[2,256,512]{2,1,0:T(8,128)(2,1)S(1)} copy-done((bf16[2,256,512]{2,1,0:T(8,128)(2,1)S(1)}, bf16[2,256,512]{2,1,0:T(8,128)(2,1)}, u32[]{:S(2)}) %copy-start) | copy-done | bytes 524312
  45.9 6.2 %shard_map.111.zo_ref = f32[32,256,512]{2,1,0:T(8,128)S(1)} custom-call(bf16[2,256,512]{2,1,0:T(8,128)(2,1)S(1)} %copy-done, bf16[16,2,8,512]{3,2,1,0:T(8,128)(2,1)S(1)} %bitcast.18), custom_call_target="tpu_custom_call" | custom-call | flops 8000000000 | bytes 5000000 | tf_op jit(solution)/shard_map/pallas_call | solution.py:222
  52.1 3.2 %collective-permute-done.4.far_ref = bf16[16,8,256]{2,1,0:T(8,128)(2,1)S(1)} collective-permute-done((bf16[16,8,256]{2,1,0:T(8,128)(2,1)S(1)}, bf16[16,8,256]{2,1,0:T(8,128)(2,1)S(1)}, u32[]{:S(2)}, u32[]{:S(2)}) %collective-permute-start.4) | collective-permute-done | bytes 65568 | tf_op jit(solution)/shard_map/ppermute | solution.py:322
  55.2 3.4 %shard_map.113.z1_ref = bf16[16,128,1024]{2,1,0:T(8,128)(2,1)S(1)} custom-call(bf16[2,256,512]{2,1,0:T(8,128)(2,1)S(1)} %copy-done, bf16[16,8,256]{2,1,0:T(8,128)(2,1)S(1)} %collective-permute-done.4.far_ref, f32[32,256,512]{2,1,0:T(8,128)S(1)} %shard_map.111.zo_ref), custom_call_target="tpu_custom_call" | custom-call | flops 4000000000 | bytes 5000000 | tf_op jit(solution)/shard_map/pallas_call | solution.py:246
  58.6 0.9 collective-permute-done.3.far_ref
  59.6 3.4 %shard_map.112.z0_ref = bf16[16,128,1024]{2,1,0:T(8,128)(2,1)S(1)} custom-call(bf16[2,256,512]{2,1,0:T(8,128)(2,1)S(1)} %copy-done, bf16[16,8,256]{2,1,0:T(8,128)(2,1)S(1)} %collective-permute-done.3.far_ref, f32[32,256,512]{2,1,0:T(8,128)S(1)} %shard_map.111.zo_ref), custom_call_target="tpu_custom_call" | custom-call | flops 4000000000 | bytes 5000000 | tf_op jit(solution)/shard_map/pallas_call | solution.py:246
  63.0 0.0 copy-start.1
  63.0 0.0 copy-start.2
  63.0 0.0 collective-permute-done.1.c1a_ref
  63.0 0.0 collective-permute-done.2.c1b_ref
  63.0 0.0 collective-permute-done.c0_ref
  63.1 3.3 %shard_map.114 = bf16[16,2,128,128]{3,2,1,0:T(8,128)(2,1)S(1)} custom-call(bf16[1,128,1024]{2,1,0:T(8,128)(2,1)S(1)} %collective-permute-done.c0_ref, bf16[1,64,1024]{2,1,0:T(8,128)(2,1)S(1)} %collective-permute-done.1.c1a_ref, bf16[1,64,1024]{2,1,0:T(8,128)(2,1)S(1)} %collective-permute-done.2.c1b_ref, bf16[16,128,1024]{2,1,0:T(8,128)(2,1)S(1)} %shard_map.112.z0_ref, ...), custom_call_target="tpu_custom_call" | custom-call | flops 1200000000 | bytes 10000000 | tf_op jit(solution)/shard_map/pallas_call | solution.py:284
  66.3 32.2 %all_to_all.10.in_ref = bf16[32,128,128]{2,1,0:T(8,128)(2,1)S(1)} all-to-all(bf16[32,128,128]{2,1,0:T(8,128)(2,1)S(1)} %bitcast.16), channel_id=1, replica_groups=mesh['pair'=32,'tau'=16] {'tau'}, dimensions={0} | all-to-all | bytes 2097152 | tf_op jit(solution)/shard_map/all_to_all | solution.py:318
  98.6 0.0 copy-done.1
  98.6 0.0 copy-done.2
  98.6 2.6 %shard_map.115 = f32[32,128,128]{2,1,0:T(8,128)} custom-call(s32[32]{0:T(128)S(1)} %copy-done.1, s32[512]{0:T(512)S(1)} %copy-done.2, bf16[32,128,128]{2,1,0:T(8,128)(2,1)S(1)} %all_to_all.10.in_ref), custom_call_target="tpu_custom_call" | custom-call | flops 1000000 | bytes 3000000 | tf_op jit(solution)/shard_map/pallas_call | solution.py:306
  (1 shorter events, 0.0 us)
Async XLA Ops:
  3.1 30.5 %all-to-all-start = ((bf16[32,8,512]{2,1,0:T(8,128)(2,1)}), bf16[32,8,512]{2,1,0:T(8,128)(2,1)S(1)}, u32[]{:S(2)}, u32[]{:S(2)}) async-start(bf16[32,8,512]{2,1,0:T(8,128)(2,1)} %get-tuple-element.12), calls=%async_computation | async-start | bytes 524288 | tf_op jit(solution)/shard_map/all_to_all | solution.py:318
  10.6 52.4 %collective-permute-start.1 = (bf16[1,64,1024]{2,1,0:T(8,128)(2,1)}, bf16[1,64,1024]{2,1,0:T(8,128)(2,1)S(1)}, u32[]{:S(2)}, u32[]{:S(2)}) collective-permute-start(bf16[1,64,1024]{2,1,0:T(8,128)(2,1)} %get-tuple-element.10), channel_id=1, source_target_pairs={{0,112},{1,433},{2,178},{3,371},{4,20},{5,149},{6,278},{7,407},{8,... | collective-permute-start | bytes 393224 | tf_op jit(solution)/shard_map/ppermute | solution.py:322
  17.7 45.3 %collective-permute-start.2 = (bf16[1,64,1024]{2,1,0:T(8,128)(2,1)}, bf16[1,64,1024]{2,1,0:T(8,128)(2,1)S(1)}, u32[]{:S(2)}, u32[]{:S(2)}) collective-permute-start(bf16[1,64,1024]{2,1,0:T(8,128)(2,1)} %get-tuple-element.11), channel_id=1, source_target_pairs={{0,112},{1,433},{2,178},{3,371},{4,20},{5,149},{6,278},{7,407},{8,... | collective-permute-start | bytes 393224 | tf_op jit(solution)/shard_map/ppermute | solution.py:322
  28.6 34.5 %collective-permute-start = (bf16[1,128,1024]{2,1,0:T(8,128)(2,1)}, bf16[1,128,1024]{2,1,0:T(8,128)(2,1)S(1)}, u32[]{:S(2)}, u32[]{:S(2)}) collective-permute-start(bf16[1,128,1024]{2,1,0:T(8,128)(2,1)} %get-tuple-element.9), channel_id=1, source_target_pairs={{0,32},{1,225},{2,290},{3,483},{4,68},{5,453},{6,198},{7,327},{8,1... | collective-permute-start | bytes 786440 | tf_op jit(solution)/shard_map/ppermute | solution.py:322
  33.6 21.7 %collective-permute-start.4 = (bf16[16,8,256]{2,1,0:T(8,128)(2,1)S(1)}, bf16[16,8,256]{2,1,0:T(8,128)(2,1)S(1)}, u32[]{:S(2)}, u32[]{:S(2)}) collective-permute-start(bf16[16,8,256]{2,1,0:T(8,128)(2,1)S(1)} %get-tuple-element.13), channel_id=1, source_target_pairs={{0,112},{1,433},{2,178},{3,371},{4,20},{5,149},{6,278},{7,407},{8,... | collective-permute-start | bytes 196616 | tf_op jit(solution)/shard_map/ppermute | solution.py:322
  38.2 21.3 %collective-permute-start.3 = (bf16[16,8,256]{2,1,0:T(8,128)(2,1)S(1)}, bf16[16,8,256]{2,1,0:T(8,128)(2,1)S(1)}, u32[]{:S(2)}, u32[]{:S(2)}) collective-permute-start(bf16[16,8,256]{2,1,0:T(8,128)(2,1)S(1)} %get-tuple-element.14), channel_id=1, source_target_pairs={{0,32},{1,225},{2,290},{3,483},{4,68},{5,453},{6,198},{7,327},{8,1... | collective-permute-start | bytes 196616 | tf_op jit(solution)/shard_map/ppermute | solution.py:322
  44.8 1.0 %copy-start = (bf16[2,256,512]{2,1,0:T(8,128)(2,1)S(1)}, bf16[2,256,512]{2,1,0:T(8,128)(2,1)}, u32[]{:S(2)}) copy-start(bf16[2,256,512]{2,1,0:T(8,128)(2,1)} %shard_map.110.cin_ref) | copy-start | bytes 1572868
  63.0 35.6 %copy-start.1 = (s32[32]{0:T(128)S(1)}, s32[32]{0:T(128)}, u32[]{:S(2)}) copy-start(s32[32]{0:T(128)} %partner_ref.3) | copy-start | bytes 388
  63.0 35.5 %copy-start.2 = (s32[512]{0:T(512)S(1)}, s32[512]{0:T(512)}, u32[]{:S(2)}) copy-start(s32[512]{0:T(512)} %constant.14.clone.column_ref) | copy-start | bytes 6148

commit v7 on v5

--- a/solution.py
+++ b/solution.py
@@ -61,14 +61,25 @@
 SM = pl.BlockSpec(memory_space=pltpu.SMEM)
 
 
-def prepare_kernel(
-    asked_ref, dst_ref, near_ref, away_ref, peers_ref, coeff_ref, gf_ref, gb_ref, send_ref, atom0_ref,
-    atom1_ref, wide
-):
+def pick_kernel(asked_ref, dst_ref, coeff_ref, atom0_ref, atom1_ref):
     p, k = lax.axis_index("pair"), lax.axis_index("tau")
     for j, atom_ref in enumerate((atom0_ref, atom1_ref)):
         to = 2 * dst_ref[(j * CHIPS + p // 2) * N_TAU + k] + (p + j) % 2
         atom_ref[0] = coeff_ref[asked_ref[to]]
+
+
+def pick_atoms(send_atoms, coeff):
+    return pl.pallas_call(
+        pick_kernel,
+        in_specs=[SM] * 2 + [VM],
+        out_specs=[VM] * 2,
+        out_shape=[jax.ShapeDtypeStruct((1, AUX, 1024), BF16)] * 2,
+        cost_estimate=pl.CostEstimate(flops=1_000_000, bytes_accessed=2_000_000, transcendentals=0),
+    )(send_atoms, jnp.asarray(DST.reshape(-1)), coeff)
+
+
+def prepare_kernel(near_ref, away_ref, peers_ref, gf_ref, gb_ref, send_ref, wide):
+    p = lax.axis_index("pair")
     eye = lax.broadcasted_iota(jnp.int32, (32, 32), 0) == lax.broadcasted_iota(jnp.int32, (32, 32), 1)
     peers = peers_ref[...].astype(F32)
 
@@ -99,7 +110,7 @@
     send_ref[...] = wide[...].astype(BF16)
 
 
-def prepare(partner, send_atoms, coeff, fwd, bwd):
+def prepare(partner, fwd, bwd):
     sides = np.arange(N_PAIR) % 2
     near = np.zeros((N_PAIR, N_PAIR), np.float32)
     away = np.zeros((N_PAIR, N_PAIR), np.float32)
@@ -109,25 +120,12 @@
             away[p, j::2] = 2 * DST[j, p // 2] + (sides[p] ^ j)
     return pl.pallas_call(
         prepare_kernel,
-        in_specs=[SM] * 2 + [VM] * 6,
-        out_specs=[VM] * 3,
+        in_specs=[VM] * 5,
+        out_specs=VM,
         scratch_shapes=[pltpu.VMEM((32, 8, 512), F32)],
-        out_shape=[
-            jax.ShapeDtypeStruct((32, 8, 512), BF16),
-            jax.ShapeDtypeStruct((1, AUX, 1024), BF16),
-            jax.ShapeDtypeStruct((1, AUX, 1024), BF16),
-        ],
-        cost_estimate=pl.CostEstimate(flops=200_000_000, bytes_accessed=3_000_000, transcendentals=0),
-    )(
-        send_atoms,
-        jnp.asarray(DST.reshape(-1)),
-        jnp.asarray(near),
-        jnp.asarray(away),
-        partner.reshape(1, N_PAIR),
-        coeff,
-        fwd,
-        bwd,
-    )
+        out_shape=jax.ShapeDtypeStruct((32, 8, 512), BF16),
+        cost_estimate=pl.CostEstimate(flops=200_000_000, bytes_accessed=1_000_000, transcendentals=0),
+    )(jnp.asarray(near), jnp.asarray(away), partner.reshape(1, N_PAIR), fwd, bwd)
 
 
 def turn_kernel(partner_ref, homes_ref, src_ref, coeff_ref, cin_ref):
@@ -319,7 +317,8 @@
 
 
 def body(coeff, green_fwd, green_bwd, home_atom, send_atoms, partner, mirror):
-    send, atom0, atom1 = prepare(partner, send_atoms, coeff, green_fwd[:, 0, :], green_bwd[:, 0, :])
+    atom0, atom1 = pick_atoms(send_atoms, coeff)
+    send = prepare(partner, green_fwd[:, 0, :], green_bwd[:, 0, :])
     c0 = send_z(atom0, 0)
     c1 = send_z(atom1, 1)
     greens = exchange(send).reshape(N_TAU, 2, 8, 512)

time: 93.7 us -> 95.9 us (1.023)
  the two profiles are of different devices: /device:TPU:96 before, /device:TPU:224 now
where the time goes in v7:
time: 95.9 us; the launch traced here: 95.5 us
  blocking collectives  32.3 us (34%)
  Pallas kernels  25.9 us (27%)
  starting transfers between devices  24.4 us (25%)
  waiting for transfers between devices  11.7 us (12%)
  local copies, waits for them, and re-layouts  1.06 us (1%)
    all_to_all x1, blocking collectives, exchange(): return lax.all_to_all(x, 'tau', split_axis=0, concat_axis=0, tiled=True)  32.3 us
    ppermute x4, starting transfers between devices, send_z(): return lax.ppermute(x, BOTH, PERMS[j])  17.4 us
    ppermute x4, waiting for transfers between devices, send_z(): return lax.ppermute(x, BOTH, PERMS[j])  11.7 us
    all_to_all x1, starting transfers between devices, exchange(): return lax.all_to_all(x, 'tau', split_axis=0, concat_axis=0, tiled=True)  7.03 us
    pallas_call x2, Pallas kernels, far_half(): pl.pallas_call(functools.partial(far_kernel, slot), in_specs=[VM] * 3, ou...  6.84 us
    pallas_call x1, Pallas kernels, own_half(): pl.pallas_call(own_kernel, in_specs=[VM] * 2, out_specs=VM, scratch_shape...  6.18 us
    pallas_call x1, Pallas kernels, last_product(): pl.pallas_call(last_kernel, in_specs=[VM] * 4, out_specs=VM, scratch_shap...  3.26 us
    pallas_call x1, Pallas kernels, prepare(): pl.pallas_call(prepare_kernel, in_specs=[VM] * 5, out_specs=VM, scratch_s...  2.62 us
  transfers between devices with their start and end apart: 5, of which 1 were waited for; matrix products, arithmetic and copies ran while one was open for 0% of the time, Pallas kernels for 18%

profile of v7, /device:TPU:224, one launch (start us, length us, event | category | flops | bytes accessed | tf_op | source)
XLA Modules:
  0.0 95.5 jit_solution(11521912269277162066)
XLA Ops:
  0.0 2.6 %shard_map.111 = bf16[32,8,512]{2,1,0:T(8,128)(2,1)} custom-call(f32[32,32]{1,0:T(8,128)} %constant.11.clone.near_ref, f32[32,32]{1,0:T(8,128)} %constant.12.clone.away_ref, s32[1,32]{1,0:T(1,128)} %bitcast.19, bf16[32,1024]{1,0:T(8,128)(2,1)} %bitcast.20, bf16[32,1024]{1,0:T(8,128)(2,1)} %bitcast.21), custom_call_target="tpu_custom_call" | custom-call | flops 200000000 | bytes 1000000 | tf_op jit(solution)/shard_map/pallas_call | solution.py:121
  2.6 7.0 %all-to-all-start = ((bf16[32,8,512]{2,1,0:T(8,128)(2,1)}), bf16[32,8,512]{2,1,0:T(8,128)(2,1)S(1)}, u32[]{:S(2)}, u32[]{:S(2)}) async-start(bf16[32,8,512]{2,1,0:T(8,128)(2,1)} %shard_map.111), calls=%async_computation | async-start | bytes 524288 | tf_op jit(solution)/shard_map/all_to_all | solution.py:312
  9.7 2.1 %shard_map.109 = (bf16[1,128,1024]{2,1,0:T(8,128)(2,1)}, bf16[1,128,1024]{2,1,0:T(8,128)(2,1)}) custom-call(s32[32]{0:T(128)} %asked_ref.1, s32[512]{0:T(512)} %constant.10.clone.dst_ref, bf16[4,128,1024]{2,1,0:T(8,128)(2,1)} %coeff_ref.3), custom_call_target="tpu_custom_call" | custom-call | flops 1000000 | bytes 2000000 | tf_op jit(solution)/shard_map/pallas_call | solution.py:72
  11.7 2.0 %collective-permute-start = (bf16[1,128,1024]{2,1,0:T(8,128)(2,1)}, bf16[1,128,1024]{2,1,0:T(8,128)(2,1)S(1)}, u32[]{:S(2)}, u32[]{:S(2)}) collective-permute-start(bf16[1,128,1024]{2,1,0:T(8,128)(2,1)} %get-tuple-element.7), channel_id=1, source_target_pairs={{0,32},{1,225},{2,290},{3,483},{4,68},{5,453},{6,198},{7,327},{8,1... | collective-permute-start | bytes 786440 | tf_op jit(solution)/shard_map/ppermute | solution.py:316
  13.8 6.6 %collective-permute-start.1 = (bf16[1,128,1024]{2,1,0:T(8,128)(2,1)}, bf16[1,128,1024]{2,1,0:T(8,128)(2,1)S(1)}, u32[]{:S(2)}, u32[]{:S(2)}) collective-permute-start(bf16[1,128,1024]{2,1,0:T(8,128)(2,1)} %get-tuple-element.8), channel_id=1, source_target_pairs={{0,112},{1,433},{2,178},{3,371},{4,20},{5,149},{6,278},{7,407},{8,... | collective-permute-start | bytes 786440 | tf_op jit(solution)/shard_map/ppermute | solution.py:316
  20.4 2.3 %shard_map.110.cin_ref = bf16[2,256,512]{2,1,0:T(8,128)(2,1)} custom-call(s32[32]{0:T(128)} %partner_ref.3, s32[32]{0:T(128)} %homes_ref.1, s32[512]{0:T(512)} %constant.13.clone.src_ref, bf16[4,128,1024]{2,1,0:T(8,128)(2,1)} %coeff_ref.3), custom_call_target="tpu_custom_call" | custom-call | flops 100000000 | bytes 2000000 | tf_op jit(solution)/shard_map/pallas_call | solution.py:144
  22.7 0.0 all-to-all-done
  22.7 6.8 %collective-permute-start.2 = (bf16[16,8,256]{2,1,0:T(8,128)(2,1)S(1)}, bf16[16,8,256]{2,1,0:T(8,128)(2,1)S(1)}, u32[]{:S(2)}, u32[]{:S(2)}) collective-permute-start(bf16[16,8,256]{2,1,0:T(8,128)(2,1)S(1)} %get-tuple-element.10), channel_id=1, source_target_pairs={{0,32},{1,225},{2,290},{3,483},{4,68},{5,453},{6,198},{7,327},{8,1... | collective-permute-start | bytes 196616 | tf_op jit(solution)/shard_map/ppermute | solution.py:316
  29.6 0.0 copy-start
  29.6 1.0 %copy-done = bf16[2,256,512]{2,1,0:T(8,128)(2,1)S(1)} copy-done((bf16[2,256,512]{2,1,0:T(8,128)(2,1)S(1)}, bf16[2,256,512]{2,1,0:T(8,128)(2,1)}, u32[]{:S(2)}) %copy-start) | copy-done | bytes 524312
  30.6 6.2 %shard_map.112.zo_ref = f32[32,256,512]{2,1,0:T(8,128)S(1)} custom-call(bf16[2,256,512]{2,1,0:T(8,128)(2,1)S(1)} %copy-done, bf16[16,2,8,512]{3,2,1,0:T(8,128)(2,1)S(1)} %bitcast.18), custom_call_target="tpu_custom_call" | custom-call | flops 8000000000 | bytes 5000000 | tf_op jit(solution)/shard_map/pallas_call | solution.py:217
  36.8 1.9 %collective-permute-start.3 = (bf16[16,8,256]{2,1,0:T(8,128)(2,1)S(1)}, bf16[16,8,256]{2,1,0:T(8,128)(2,1)S(1)}, u32[]{:S(2)}, u32[]{:S(2)}) collective-permute-start(bf16[16,8,256]{2,1,0:T(8,128)(2,1)S(1)} %get-tuple-element.9), channel_id=1, source_target_pairs={{0,112},{1,433},{2,178},{3,371},{4,20},{5,149},{6,278},{7,407},{8,... | collective-permute-start | bytes 196616 | tf_op jit(solution)/shard_map/ppermute | solution.py:316
  38.7 11.7 %collective-permute-done.2.far_ref = bf16[16,8,256]{2,1,0:T(8,128)(2,1)S(1)} collective-permute-done((bf16[16,8,256]{2,1,0:T(8,128)(2,1)S(1)}, bf16[16,8,256]{2,1,0:T(8,128)(2,1)S(1)}, u32[]{:S(2)}, u32[]{:S(2)}) %collective-permute-start.2) | collective-permute-done | bytes 65568 | tf_op jit(solution)/shard_map/ppermute | solution.py:316
  50.4 3.4 %shard_map.113.z0_ref = bf16[16,128,1024]{2,1,0:T(8,128)(2,1)S(1)} custom-call(bf16[2,256,512]{2,1,0:T(8,128)(2,1)S(1)} %copy-done, bf16[16,8,256]{2,1,0:T(8,128)(2,1)S(1)} %collective-permute-done.2.far_ref, f32[32,256,512]{2,1,0:T(8,128)S(1)} %shard_map.112.zo_ref), custom_call_target="tpu_custom_call" | custom-call | flops 4000000000 | bytes 5000000 | tf_op jit(solution)/shard_map/pallas_call | solution.py:241
  53.9 0.0 collective-permute-done.3.far_ref
  53.9 3.4 %shard_map.114.z1_ref = bf16[16,128,1024]{2,1,0:T(8,128)(2,1)S(1)} custom-call(bf16[2,256,512]{2,1,0:T(8,128)(2,1)S(1)} %copy-done, bf16[16,8,256]{2,1,0:T(8,128)(2,1)S(1)} %collective-permute-done.3.far_ref, f32[32,256,512]{2,1,0:T(8,128)S(1)} %shard_map.112.zo_ref), custom_call_target="tpu_custom_call" | custom-call | flops 4000000000 | bytes 5000000 | tf_op jit(solution)/shard_map/pallas_call | solution.py:241
  57.3 0.0 copy-start.1
  57.3 0.0 copy-start.2
  57.3 0.0 collective-permute-done.c0_ref
  57.3 0.0 collective-permute-done.1.c1_ref
  57.3 3.3 %shard_map.115 = bf16[16,2,128,128]{3,2,1,0:T(8,128)(2,1)S(1)} custom-call(bf16[1,128,1024]{2,1,0:T(8,128)(2,1)S(1)} %collective-permute-done.c0_ref, bf16[1,128,1024]{2,1,0:T(8,128)(2,1)S(1)} %collective-permute-done.1.c1_ref, bf16[16,128,1024]{2,1,0:T(8,128)(2,1)S(1)} %shard_map.113.z0_ref, bf16[16,128,1024]{2,1,0:T(8,128)(2,1)S(1)} %shard_map.114.z1_ref), custom_call_target="tpu_custom_call" | custom-call | flops 1200000000 | bytes 10000000 | tf_op jit(solution)/shard_map/pallas_call | solution.py:278
  60.6 32.3 %all_to_all.10.in_ref = bf16[32,128,128]{2,1,0:T(8,128)(2,1)S(1)} all-to-all(bf16[32,128,128]{2,1,0:T(8,128)(2,1)S(1)} %bitcast.16), channel_id=1, replica_groups=mesh['pair'=32,'tau'=16] {'tau'}, dimensions={0} | all-to-all | bytes 2097152 | tf_op jit(solution)/shard_map/all_to_all | solution.py:312
  92.9 0.0 copy-done.1
  92.9 0.0 copy-done.2
  92.9 2.6 %shard_map.116 = f32[32,128,128]{2,1,0:T(8,128)} custom-call(s32[32]{0:T(128)S(1)} %copy-done.2, s32[512]{0:T(512)S(1)} %copy-done.1, bf16[32,128,128]{2,1,0:T(8,128)(2,1)S(1)} %all_to_all.10.in_ref), custom_call_target="tpu_custom_call" | custom-call | flops 1000000 | bytes 3000000 | tf_op jit(solution)/shard_map/pallas_call | solution.py:300
  (1 shorter events, 0.0 us)
Async XLA Ops:
  2.6 20.1 %all-to-all-start = ((bf16[32,8,512]{2,1,0:T(8,128)(2,1)}), bf16[32,8,512]{2,1,0:T(8,128)(2,1)S(1)}, u32[]{:S(2)}, u32[]{:S(2)}) async-start(bf16[32,8,512]{2,1,0:T(8,128)(2,1)} %shard_map.111), calls=%async_computation | async-start | bytes 524288 | tf_op jit(solution)/shard_map/all_to_all | solution.py:312
  11.7 45.6 %collective-permute-start = (bf16[1,128,1024]{2,1,0:T(8,128)(2,1)}, bf16[1,128,1024]{2,1,0:T(8,128)(2,1)S(1)}, u32[]{:S(2)}, u32[]{:S(2)}) collective-permute-start(bf16[1,128,1024]{2,1,0:T(8,128)(2,1)} %get-tuple-element.7), channel_id=1, source_target_pairs={{0,32},{1,225},{2,290},{3,483},{4,68},{5,453},{6,198},{7,327},{8,1... | collective-permute-start | bytes 786440 | tf_op jit(solution)/shard_map/ppermute | solution.py:316
  13.8 43.6 %collective-permute-start.1 = (bf16[1,128,1024]{2,1,0:T(8,128)(2,1)}, bf16[1,128,1024]{2,1,0:T(8,128)(2,1)S(1)}, u32[]{:S(2)}, u32[]{:S(2)}) collective-permute-start(bf16[1,128,1024]{2,1,0:T(8,128)(2,1)} %get-tuple-element.8), channel_id=1, source_target_pairs={{0,112},{1,433},{2,178},{3,371},{4,20},{5,149},{6,278},{7,407},{8,... | collective-permute-start | bytes 786440 | tf_op jit(solution)/shard_map/ppermute | solution.py:316
  22.7 27.7 %collective-permute-start.2 = (bf16[16,8,256]{2,1,0:T(8,128)(2,1)S(1)}, bf16[16,8,256]{2,1,0:T(8,128)(2,1)S(1)}, u32[]{:S(2)}, u32[]{:S(2)}) collective-permute-start(bf16[16,8,256]{2,1,0:T(8,128)(2,1)S(1)} %get-tuple-element.10), channel_id=1, source_target_pairs={{0,32},{1,225},{2,290},{3,483},{4,68},{5,453},{6,198},{7,327},{8,1... | collective-permute-start | bytes 196616 | tf_op jit(solution)/shard_map/ppermute | solution.py:316
  29.6 1.0 %copy-start = (bf16[2,256,512]{2,1,0:T(8,128)(2,1)S(1)}, bf16[2,256,512]{2,1,0:T(8,128)(2,1)}, u32[]{:S(2)}) copy-start(bf16[2,256,512]{2,1,0:T(8,128)(2,1)} %shard_map.110.cin_ref) | copy-start | bytes 1572868
  36.8 17.1 %collective-permute-start.3 = (bf16[16,8,256]{2,1,0:T(8,128)(2,1)S(1)}, bf16[16,8,256]{2,1,0:T(8,128)(2,1)S(1)}, u32[]{:S(2)}, u32[]{:S(2)}) collective-permute-start(bf16[16,8,256]{2,1,0:T(8,128)(2,1)S(1)} %get-tuple-element.9), channel_id=1, source_target_pairs={{0,112},{1,433},{2,178},{3,371},{4,20},{5,149},{6,278},{7,407},{8,... | collective-permute-start | bytes 196616 | tf_op jit(solution)/shard_map/ppermute | solution.py:316
  57.3 35.6 %copy-start.1 = (s32[512]{0:T(512)S(1)}, s32[512]{0:T(512)}, u32[]{:S(2)}) copy-start(s32[512]{0:T(512)} %constant.14.clone.column_ref) | copy-start | bytes 6148
  57.3 35.6 %copy-start.2 = (s32[32]{0:T(128)S(1)}, s32[32]{0:T(128)}, u32[]{:S(2)}) copy-start(s32[32]{0:T(128)} %partner_ref.3) | copy-start | bytes 388
